TPU v7x, 32 devices: a whole 2x2x4 slice. The times are simulated.
32 devices in a mesh: seq: 8 (over z, y), chan: 4 (over x, core).
Axes of the slice: x: 2, y: 2, z: 4, core: 2. Of those that a mesh axis runs over, the one named last changes fastest.
Arguments:
- inputs: bfloat16 [4096, 4096], P('seq', 'chan'), may hold values from -6 to 6
- out_grad: bfloat16 [4096, 4096], P('seq', 'chan'), may hold values from -0.0048828125 to 0.0048828125
- embed_weight: float32 [17, 64], replicated, may hold values from -1.5 to 1.5
- embed_bias: float32 [64], replicated, may hold values from -1 to 1
- embed_freq: float32 [64], replicated, may hold values from 0.5 to 2
- mixer_weight: float32 [64, 64], replicated, may hold values from -0.75 to 0.75
- mixer_bias: float32 [64], replicated, may hold values from -1 to 1
- mixer_freq: float32 [64], replicated, may hold values from 0.5 to 2
- head_weight: float32 [64, 4096], P(None, 'chan'), may hold values from -0.75 to 0.75
- decay_rates: float32 [4096], P('chan'), may hold values from 1 to 12
Outputs:
- embed_weight_grad: float32 [17, 64], replicated
- embed_bias_grad: float32 [64], replicated
- embed_freq_grad: float32 [64], replicated
- mixer_weight_grad: float32 [64, 64], replicated
- mixer_bias_grad: float32 [64], replicated
- mixer_freq_grad: float32 [64], replicated
- head_weight_grad: float32 [64, 4096], P(None, 'chan')
- decay_rates_grad: float32 [4096], P('chan')
All inputs are finite; a program needn't handle non-finite values.
Results may differ from a plain program's by a relative error of at most 0.0003.
Values may be sent and summed in bfloat16 or wider, within the bound.
No kernel may reach another device: no remote copies, remote signals or barrier semaphores. Data moves between devices by JAX's collectives and lax.ppermute only.
A program may use at most 128 MiB of HBM per device.

v0:
```python
import functools
import math

import jax
import jax.numpy as jnp
import numpy as np
from jax import lax
from jax.experimental import pallas as pl
from jax.experimental.pallas import tpu as pltpu
from jax.sharding import PartitionSpec as P


BANDS = 8
SPAN_PARTS = 3
EXACT = lax.Precision.HIGHEST


def swapped(value, axis, bit):
    return lax.ppermute(value, axis, [(i, i ^ bit) for i in range(lax.axis_size(axis))])


def bits_of(axis, first=1):
    count = lax.axis_size(axis)
    assert count & (count - 1) == 0
    return [1 << i for i in range(count.bit_length() - 1) if (1 << i) >= first]


def split_const(matrix):
    high = matrix.astype(np.float32).astype(jnp.bfloat16)
    low = (matrix - high.astype(np.float64)).astype(np.float32).astype(jnp.bfloat16)
    return high, low


@functools.cache
def transforms(size):
    freqs = np.arange(0, size, 2)
    freqs = np.concatenate([freqs, size - 1 - freqs])
    omega = np.pi * (2 * freqs + 1) / (2 * size)
    steps = np.arange(size)
    forward = np.concatenate(
        [np.cos(omega[:, None] * steps), -np.sin(omega[:, None] * steps)], axis=0
    )
    omega = omega[: size // 2]
    dist = size - tap_order(size)
    inverse = (
        np.concatenate(
            [np.cos(dist[:, None] * omega), -np.sin(dist[:, None] * omega)], axis=1
        )
        / size
    )
    return split_const(forward), split_const(inverse)


def tap_order(size):
    return np.concatenate([np.arange(0, size, 2), np.arange(1, size, 2)])


def split_pair(value):
    high = value.astype(jnp.bfloat16)
    return high, (value - high.astype(jnp.float32)).astype(jnp.bfloat16)


@functools.cache
def tap_features(filter_len, size, band_count):
    tap = np.concatenate([m * size + tap_order(size) for m in range(filter_len // size)])
    scaled = tap.astype(np.float32) / np.float32(filter_len)
    rates = [max(1, filter_len // 4 // 2 ** (band_count - i)) for i in range(1, band_count + 1)]
    cycles = np.array(rates)[:, None] * tap[None, :] % filter_len
    angle = cycles.astype(np.float32) * np.float32(2.0 * math.pi / filter_len)
    angle = angle.astype(np.float64)
    return np.concatenate([scaled[None, :], np.cos(angle), np.sin(angle)], axis=0).astype(
        np.float32
    )


def dot32(left, right, dims=(((1,), (0,)), ((), ()))):
    return lax.dot_general(
        left, right, dims, precision=EXACT, preferred_element_type=jnp.float32
    )


def dot16(left, right, dims=(((1,), (0,)), ((), ()))):
    return lax.dot_general(left, right, dims, preferred_element_type=jnp.float32)


NT = (((1,), (1,)), ((), ()))
FIXED, BEYOND, WINDOWED = 0, 4, 6


def block_pairs(groups):
    return [(b, j, b + 4 - j) for j in range(8) for b in range(4) if 0 <= b + 4 - j < groups]


TN = (((0,), (0,)), ((), ()))
SIN_TERMS = [(-1.0) ** i / math.factorial(2 * i + 1) for i in range(6)]
COS_TERMS = [(-1.0) ** i / math.factorial(2 * i) for i in range(7)]


def sine_cosine(angle):
    turns = jnp.floor(angle * (1.0 / math.pi) + 0.5)
    rest = angle - turns * 3.140625
    rest = rest - turns * 9.67502593994140625e-4
    rest = rest - turns * 1.509957990978376432e-7
    sign = 1.0 - 4.0 * (0.5 * turns - jnp.floor(0.5 * turns))
    square = rest * rest
    sine = SIN_TERMS[-1]
    for term in SIN_TERMS[-2::-1]:
        sine = sine * square + term
    cosine = COS_TERMS[-1]
    for term in COS_TERMS[-2::-1]:
        cosine = cosine * square + term
    return sine * (rest * sign), cosine * sign


def prep_kernel(
    ew_ref,
    eb_ref,
    ef_ref,
    mw_ref,
    mb_ref,
    mf_ref,
    feats_ref,
    acth_ref,
    actl_ref,
    pre1_ref,
    act1_ref,
    cos1_ref,
    pre2_ref,
    cos2_ref,
    cols_ref,
):
    hidden = mw_ref.shape[0]
    vectors = jnp.concatenate(
        [eb_ref[...], ef_ref[...], mb_ref[...], mf_ref[...]] * 2, axis=0
    )
    vectors = jnp.concatenate([vectors, jnp.zeros_like(vectors)], axis=1).T
    cols_ref[...] = vectors[:hidden]
    first_pre = dot32(ew_ref[...], feats_ref[...], TN) + cols_ref[:, 0:1]
    first_act, first_cos = sine_cosine(first_pre * cols_ref[:, 1:2])
    pre1_ref[...] = first_pre
    act1_ref[...] = first_act
    cos1_ref[...] = first_cos
    second_pre = dot32(mw_ref[...], first_act, TN) + cols_ref[:, 2:3]
    second_act, second_cos = sine_cosine(second_pre * cols_ref[:, 3:4])
    pre2_ref[...] = second_pre
    cos2_ref[...] = second_cos
    for i, value in enumerate((second_act, second_act * feats_ref[0:1, :])):
        high, low = split_pair(value)
        acth_ref[i * hidden : (i + 1) * hidden, :] = high
        actl_ref[i * hidden : (i + 1) * hidden, :] = low


def main_kernel(
    size,
    groups,
    filter_len,
    first,
    last,
    chunk,
    par_ref,
    xk_ref,
    gk_ref,
    e1_ref,
    e2_ref,
    za_ref,
    zb_ref,
    s3_ref,
    fwd_ref,
    inv_ref,
    acth_ref,
    actl_ref,
    head_ref,
    rates_ref,
    *rest,
):
    rest = list(rest)
    second_in = None if first else rest.pop(0)
    if last:
        net_in, rest = rest[:8], rest[8:]
        part_ref, net_ref, spec, prod, hold, second_ref = rest
    else:
        part_ref, second_ref, spec, prod, hold = rest
    par = par_ref[0]
    width = xk_ref.shape[1]
    hidden = head_ref.shape[0]
    mid = size // 2

    def transform(ref, slot):
        for i in range(2):
            block = ref[i * size : (i + 1) * size, :]
            spec[slot + (i ^ par)] = dot16(fwd_ref[par], jnp.concatenate([block, block], axis=0))

    half = head_ref.shape[1] // 2
    here = pl.ds(pl.multiple_of(par * half + chunk * width, width), width)

    transform(xk_ref, (WINDOWED + 4) * (1 - par))
    transform(gk_ref, (WINDOWED + 4) * par)
    before, beyond = WINDOWED - 2 * par, BEYOND + 2 * par
    odd = par_ref[1]
    transform(za_ref, beyond + odd * (before - beyond))
    transform(zb_ref, before + odd * (beyond - before))
    transform(e1_ref, WINDOWED + 6)
    transform(e2_ref, FIXED + 2)
    transform(s3_ref, WINDOWED + 2)

    lanes = 128
    rows = 16
    tiles = mid // rows

    def products(row, lane, sign):
        def load(slot):
            return (
                spec[slot, pl.ds(row, rows), pl.ds(lane, lanes)],
                spec[slot, pl.ds(row + size, rows), pl.ds(lane, lanes)],
            )

        acc_re = [None] * groups
        acc_im = [None] * groups

        def add(m, g, w):
            re = g[0] * w[0] + g[1] * w[1]
            im = g[0] * w[1] - g[1] * w[0]
            acc_re[m] = re if acc_re[m] is None else acc_re[m] + re
            acc_im[m] = im if acc_im[m] is None else acc_im[m] + im

        fixed = [load(FIXED + b) for b in range(4)]
        prev = None
        for j in range(8):
            now = load(WINDOWED + j)
            if prev is None:
                w = (now[1], -now[0]) if sign > 0 else (-now[1], now[0])
            elif sign > 0:
                w = (prev[0] + now[1], prev[1] - now[0])
            else:
                w = (prev[0] - now[1], prev[1] + now[0])
            for b, jj, m in block_pairs(groups):
                if jj == j:
                    add(m, fixed[b], w)
            if j == 3:
                near, far = load(BEYOND), load(BEYOND + 1)
                add(5, near, w)
                add(4, near, now)
                add(5, far, now)
            prev = now
        return acc_re, acc_im

    def body(it, carry):
        row = pl.multiple_of((it % tiles) * rows, rows)
        lane = pl.multiple_of((it // tiles) * lanes, lanes)
        even_re, even_im = products(row, lane, 1)
        for m in range(groups):
            hold[2 * m] = even_re[m]
            hold[2 * m + 1] = even_im[m]
        odd_re, odd_im = products(row + mid, lane, -1)
        for m in range(groups):
            re, im = hold[2 * m], hold[2 * m + 1]
            folded = (re + odd_re[m], im - odd_im[m], re - odd_re[m], im + odd_im[m])
            for part, value in enumerate(folded):
                high, low = split_pair(value)
                at = (pl.ds(row + part * mid, rows), pl.ds(lane, lanes))
                prod[2 * m, at[0], at[1]] = high
                prod[2 * m + 1, at[0], at[1]] = low
        return carry

    lax.fori_loop(0, tiles * (width // lanes), body, 0)

    rates = rates_ref[:, here]
    tap = lax.broadcasted_iota(jnp.int32, (size, width), 0)
    tap = jnp.where(tap < mid, 2 * tap, 2 * (tap - mid) + 1)
    inner = jnp.exp(-(tap.astype(jnp.float32) / filter_len) * rates)
    head = head_ref[:, here]
    head_high, head_low = split_pair(head)
    total = jnp.zeros((2 * hidden, width), jnp.float32)
    for m in range(groups):
        grads = []
        for q in range(2):
            high = prod[2 * m, q * size : (q + 1) * size, :]
            low = prod[2 * m + 1, q * size : (q + 1) * size, :]
            both = dot16(inv_ref[q], high)
            grads.append(both[:mid] + both[mid:] + dot16(inv_ref[q, :mid, :], low))
        outer = jnp.exp(-(m * size / filter_len) * rates)
        delta = jnp.concatenate(grads, axis=0) * (inner * outer)
        high, low = split_pair(delta)
        cols = slice(m * size, (m + 1) * size)
        total += (
            dot16(acth_ref[:, cols], high)
            + dot16(acth_ref[:, cols], low)
            + dot16(actl_ref[:, cols], high)
        )
        second = (
            dot16(head_high, high, NT) + dot16(head_high, low, NT) + dot16(head_low, high, NT)
        )
        second_ref[:, cols] = second if first else second + second_in[:, cols]

    part_ref[:hidden, :] = total[:hidden]
    part_ref[hidden:, :] = jnp.broadcast_to(
        -jnp.sum(total[hidden:] * head, axis=0, keepdims=True),
        (part_ref.shape[0] - hidden, width),
    )

    if last:
        mix, cols, feats, pre1, act1, cos1, pre2, cos2 = (r[...] for r in net_in)
        mix_freq, emb_freq = cols[:, 3:4], cols[:, 1:2]
        slope2 = second_ref[...] * cos2
        delta2 = slope2 * mix_freq
        slope1 = dot32(mix, delta2) * cos1
        delta1 = slope1 * emb_freq
        count = feats.shape[0]
        net_ref[:, :hidden] = dot32(delta2, act1, NT)
        net_ref[:, hidden : hidden + count] = dot32(delta1, feats, NT)
        for i, value in enumerate((delta1, slope1 * pre1, delta2, slope2 * pre2)):
            at = hidden + count + i
            net_ref[:, at : at + 1] = jnp.sum(value, axis=1, keepdims=True)
        at = hidden + count + 4
        net_ref[:, at:] = jnp.zeros((hidden, net_ref.shape[1] - at), jnp.float32)


def finish_kernel(count, par_ref, net_ref, far_ref, *rest):
    ew_ref, eb_ref, ef_ref, mw_ref, mb_ref, mf_ref, head_ref, rates_ref = rest[-8:]
    parts = rest[:-8]
    par = par_ref[0]
    turned = (net_ref[...] + far_ref[...]).T
    hidden = turned.shape[1]
    mw_ref[...] = turned[:hidden]
    ew_ref[...] = turned[hidden : hidden + count]
    for i, ref in enumerate((eb_ref, ef_ref, mb_ref, mf_ref)):
        ref[...] = turned[hidden + count + i : hidden + count + i + 1]
    width = parts[0].shape[1]
    half = head_ref.shape[1] // 2
    for i in range(len(parts) // 2):
        for which, ref in ((par, parts[2 * i]), (1 - par, parts[2 * i + 1])):
            at = pl.ds(pl.multiple_of(which * half + i * width, width), width)
            head_ref[:, at] = ref[:hidden, :]
            rates_ref[:, at] = ref[hidden : hidden + 1, :]


def after(value, *others):
    return lax.optimization_barrier((value, *others))[0]


def work(
    inputs,
    out_grad,
    embed_weight,
    embed_bias,
    embed_freq,
    mixer_weight,
    mixer_bias,
    mixer_freq,
    head_weight,
    decay_rates,
):
    block_len, chan_count = inputs.shape
    hidden = head_weight.shape[0]
    half = chan_count // 2
    size = block_len // 2
    filter_len = SPAN_PARTS * block_len
    groups = filter_len // size
    par = lax.axis_index("seq") % 2
    count = lax.axis_size("seq")
    width = min(256, half)
    chunks = range(half // width)

    def part_of(value, which, chunk, span):
        start = which * half + chunk * span
        return lax.dynamic_slice_in_dim(value, start, span, axis=1)

    def gives(inputs, out_grad, chunk):
        x_give = part_of(inputs, 1 - par, chunk, width)
        g_give = part_of(out_grad, 1 - par, chunk, width)
        return jnp.where(par == 0, g_give, x_give), jnp.where(par == 0, x_give, g_give)

    odd = (lax.axis_index("seq") // 2) % 2
    place = jnp.stack([par, odd]).astype(jnp.int32)
    ahead = [(i, i + 2) for i in range(0, count - 2, 2)]
    back = [(i, i - 2) for i in range(3, count, 2)]
    upper = [i for i in range(count - 2) if (i // 2) % 2 == 1]
    middle = [(i, i + 2) for i in upper] + [(i + 2, i) for i in upper]
    one0, _ = gives(inputs, out_grad, 0)
    e1 = [swapped(one0, "seq", 1)]
    own_in, own_grad, _ = lax.optimization_barrier((inputs, out_grad, one0))
    x_keep = part_of(own_in, par, 0, half)
    g_keep = part_of(own_grad, par, 0, half)
    za = swapped(jnp.where(odd == 0, x_keep, g_keep), "seq", 2)
    zb = lax.ppermute(jnp.where(odd == 0, g_keep, x_keep), "seq", middle)
    own_in, own_grad, _ = lax.optimization_barrier((own_in, own_grad, x_keep))
    sends = [gives(own_in, own_grad, c) for c in chunks]
    e2, s3 = [], []
    for c in chunks[1:]:
        e1.append(swapped(after(sends[c][0], e1[-1]), "seq", 1))
    for c in chunks:
        s3.append(lax.ppermute(e1[c], "seq", ahead + back))
    for c in chunks:
        e2.append(swapped(after(sends[c][1], e1[-1] if c == 0 else e2[-1]), "seq", 1))

    features = jnp.asarray(tap_features(filter_len, size, BANDS))
    feats = features.shape[0]
    taps = jax.ShapeDtypeStruct((hidden, filter_len), jnp.float32)
    wide = jax.ShapeDtypeStruct((2 * hidden, filter_len), jnp.bfloat16)
    vmem = pl.BlockSpec(memory_space=pltpu.VMEM)
    made = pl.pallas_call(
        prep_kernel,
        in_specs=[vmem] * 7,
        out_specs=[vmem] * 8,
        out_shape=[wide, wide] + [taps] * 5 + [jax.ShapeDtypeStruct((hidden, 8), jnp.float32)],
        name="prep",
    )(
        after(embed_weight, e1[0]),
        embed_bias[None, :],
        embed_freq[None, :],
        mixer_weight,
        mixer_bias[None, :],
        mixer_freq[None, :],
        features,
    )
    act_high, act_low, first_pre, first_act, first_cos, second_pre, second_cos, cols = made

    (fwd_high, fwd_low), (inv_high, inv_low) = transforms(size)
    forward = np.concatenate([fwd_high, fwd_low], axis=1)
    mirrored = np.concatenate([forward[:size], -forward[size:]], axis=0)
    forward = jnp.asarray(np.stack([forward, mirrored]))
    mid = size // 2
    inverse = jnp.asarray(
        np.stack(
            [
                np.concatenate([inv_high[q * mid : (q + 1) * mid], inv_low[q * mid : (q + 1) * mid]])
                for q in range(2)
            ]
        )
    )

    parts = []
    second_grad = None
    for c in chunks:
        first, last = c == 0, c == chunks[-1]
        here = slice(c * width, (c + 1) * width)
        operands = [
            place,
            x_keep[:, here],
            g_keep[:, here],
            e1[c],
            e2[c],
            za[:, here],
            zb[:, here],
            s3[c],
            forward,
            inverse,
            act_high,
            act_low,
            head_weight,
            decay_rates[None, :],
        ]
        if not first:
            operands.append(second_grad)
        part_shape = jax.ShapeDtypeStruct((hidden + 8, width), jnp.float32)
        second_shape = jax.ShapeDtypeStruct((hidden, filter_len), jnp.float32)
        scratch = [
            pltpu.VMEM((14, 2 * size, width), jnp.float32),
            pltpu.VMEM((2 * groups, 2 * size, width), jnp.bfloat16),
            pltpu.VMEM((2 * groups, 16, 128), jnp.float32),
        ]
        if last:
            operands += [
                mixer_weight,
                cols,
                features,
                first_pre,
                first_act,
                first_cos,
                second_pre,
                second_cos,
            ]
            out_shape = [part_shape, jax.ShapeDtypeStruct((hidden, 2 * hidden), jnp.float32)]
            scratch.append(pltpu.VMEM((hidden, filter_len), jnp.float32))
        else:
            out_shape = [part_shape, second_shape]
        part, out = pl.pallas_call(
            functools.partial(main_kernel, size, groups, filter_len, first, last, c),
            in_specs=[pl.BlockSpec(memory_space=pltpu.SMEM)]
            + [pl.BlockSpec(memory_space=pltpu.VMEM)] * (len(operands) - 1),
            out_specs=[pl.BlockSpec(memory_space=pltpu.VMEM)] * 2,
            out_shape=out_shape,
            scratch_shapes=scratch,
            compiler_params=pltpu.CompilerParams(vmem_limit_bytes=40 * 2**20),
            cost_estimate=pl.CostEstimate(
                flops=4 * 10**9, bytes_accessed=8 * 2**20, transcendentals=0
            ),
            name="filter_grad",
        )(*operands)
        parts.append(part)
        if last:
            net = out
        else:
            second_grad = out

    far_bits = bits_of("seq", 2)
    steps = [("chan", b) for b in bits_of("chan")] + [("seq", b) for b in far_bits]
    for axis, bit in steps:
        net = net + swapped(net, axis, bit)
    far = swapped(net, "seq", 1)
    both = []
    for p in parts:
        for bit in far_bits:
            p = p + swapped(p, "seq", bit)
        both += [p, swapped(p, "seq", 1)]

    row = jax.ShapeDtypeStruct((1, hidden), jnp.float32)
    outs = pl.pallas_call(
        functools.partial(finish_kernel, feats),
        in_specs=[pl.BlockSpec(memory_space=pltpu.SMEM)]
        + [pl.BlockSpec(memory_space=pltpu.VMEM)] * (2 + len(both)),
        out_specs=[pl.BlockSpec(memory_space=pltpu.VMEM)] * 8,
        out_shape=[
            jax.ShapeDtypeStruct((feats, hidden), jnp.float32),
            row,
            row,
            jax.ShapeDtypeStruct((hidden, hidden), jnp.float32),
            row,
            row,
            jax.ShapeDtypeStruct((hidden, chan_count), jnp.float32),
            jax.ShapeDtypeStruct((1, chan_count), jnp.float32),
        ],
        name="finish",
    )(place, net, far, *both)
    return tuple(o[0] if o.shape[0] == 1 else o for o in outs)


def solution(mesh):
    in_specs = (
        P("seq", "chan"),
        P("seq", "chan"),
        P(),
        P(),
        P(),
        P(),
        P(),
        P(),
        P(None, "chan"),
        P("chan"),
    )
    out_specs = (P(), P(), P(), P(), P(), P(), P(None, "chan"), P("chan"))
    return jax.shard_map(work, mesh=mesh, in_specs=in_specs, out_specs=out_specs, check_vma=False)
```

profile of v0, /device:TPU:0, one launch (start us, length us, event | category | flops | bytes accessed | tf_op | source)
XLA Modules:
  0.0 77.9 jit_solution(18253616745459132089)
XLA Ops:
  0.7 1.1 %dynamic-slice_select_fusion.1 = bf16[512,256]{1,0:T(8,128)(2,1)S(1)} fusion(bf16[512,1024]{1,0:T(8,128)(2,1)} %param.13, s32[]{:T(128)S(6)} %select_n.65, bf16[512,1024]{1,0:T(8,128)(2,1)} %param.14, pred[]{:T(512)S(6)} %eq.7), kind=kLoop, calls=%fused_computation.3 | loop fusion | flops 131072 | bytes 786437 | tf_op jit(solution)/shard_map/jit(_where)/select_n | solution.py:371
  1.8 3.1 %collective-permute-start = (bf16[512,256]{1,0:T(8,128)(2,1)S(1)}, bf16[512,256]{1,0:T(8,128)(2,1)S(1)}, u32[]{:S(2)}, u32[]{:S(2)}) collective-permute-start(bf16[512,256]{1,0:T(8,128)(2,1)S(1)} %dynamic-slice_select_fusion.1), channel_id=1, source_target_pairs={{0,4},{4,0},{8,12},{12,8},{16,20},{20,16},{24,28},{28,24},{1,5},{5... | collective-permute-start | bytes 786440 | tf_op jit(solution)/shard_map/ppermute | solution.py:19
  4.8 2.5 %broadcast_select_fusion = (bf16[512,512]{1,0:T(8,128)(2,1)}, bf16[512,512]{1,0:T(8,128)(2,1)}) fusion(pred[]{:T(512)S(6)} %eq.14, bf16[512,1024]{1,0:T(8,128)(2,1)} %param.14, s32[]{:T(128)S(6)} %select_n.67, bf16[512,1024]{1,0:T(8,128)(2,1)} %param.13), kind=kLoop, calls=%fused_computation | loop fusion | flops 524288 | bytes 2097157 | tf_op jit(solution)/shard_map/jit(_where)/select_n | solution.py:385
  7.3 1.5 %collective-permute-start.5 = (bf16[512,512]{1,0:T(8,128)(2,1)}, bf16[512,512]{1,0:T(8,128)(2,1)}, u32[]{:S(2)}, u32[]{:S(2)}) collective-permute-start(bf16[512,512]{1,0:T(8,128)(2,1)} %get-tuple-element.64), channel_id=1, source_target_pairs={{8,16},{12,20},{16,8},{20,12},{9,17},{13,21},{17,9},{21,13},{10,18... | collective-permute-start | bytes 1572872 | tf_op jit(solution)/shard_map/ppermute | solution.py:385
  8.8 3.6 %collective-permute-start.4 = (bf16[512,512]{1,0:T(8,128)(2,1)}, bf16[512,512]{1,0:T(8,128)(2,1)S(1)}, u32[]{:S(2)}, u32[]{:S(2)}) collective-permute-start(bf16[512,512]{1,0:T(8,128)(2,1)} %get-tuple-element.65), channel_id=1, source_target_pairs={{0,8},{4,12},{8,0},{12,4},{16,24},{20,28},{24,16},{28,20},{1,9},{5... | collective-permute-start | bytes 1572872 | tf_op jit(solution)/shard_map/ppermute | solution.py:19
  12.5 0.0 copy-done.15
  12.5 0.0 copy-done.16
  12.5 1.1 %dynamic-slice_select_fusion = (bf16[512,256]{1,0:T(8,128)(2,1)}, bf16[512,256]{1,0:T(8,128)(2,1)}, bf16[512,256]{1,0:T(8,128)(2,1)}) fusion(bf16[512,1024]{1,0:T(8,128)(2,1)S(1)} %copy-done.16, s32[]{:T(128)S(6)} %select_n.65, bf16[512,1024]{1,0:T(8,128)(2,1)S(1)} %copy-done.15, pred[]{:T(512)S(6)} %eq.7, s32[]{:T(128)S(6)} %select_n.68), kind=kLoop, calls=%fused_computation.2 | loop fusion | flops 393216 | bytes 1835017 | tf_op jit(solution)/shard_map/jit(_where)/select_n | solution.py:371
  13.6 0.0 collective-permute-done.e1_ref
  13.6 0.5 collective-permute-start.1
  14.1 0.1 pad_add_fusion.par_ref
  14.2 1.2 %constant_dynamic-slice_fusion = (bf16[512,256]{1,0:T(8,128)(2,1)S(1)}, bf16[512,256]{1,0:T(8,128)(2,1)S(1)}, bf16[512,256]{1,0:T(8,128)(2,1)S(1)}, bf16[512,256]{1,0:T(8,128)(2,1)S(1)}) fusion(bf16[512,1024]{1,0:T(8,128)(2,1)S(1)} %copy-done.15, s32[]{:T(128)S(6)} %select_n.67, s32[]{:T(128)S(6)} %add.67, bf16[512,1024]{1,0:T(8,128)(2,1)} %param.14), kind=kLoop, calls=%fused_computation.6 | loop fusion | bytes 2097160 | tf_op jit(solution)/shard_map/slice | solution.py:439
  15.4 4.0 %prep.1 = (bf16[128,1536]{1,0:T(8,128)(2,1)}, bf16[128,1536]{1,0:T(8,128)(2,1)}, f32[64,1536]{1,0:T(8,128)}, f32[64,1536]{1,0:T(8,128)}, f32[64,1536]{1,0:T(8,12...) custom-call(f32[17,64]{1,0:T(8,128)} %ew_ref, f32[1,64]{1,0:T(1,128)} %bitcast.14, f32[1,64]{1,0:T(1,128)} %bitcast.15, ...), custom_call_target="tpu_custom_call" | custom-call | tf_op jit(solution)/shard_map/prep/pallas_call | solution.py:401
  19.3 2.2 %collective-permute-start.7 = (bf16[512,256]{1,0:T(8,128)(2,1)S(1)}, bf16[512,256]{1,0:T(8,128)(2,1)S(1)}, u32[]{:S(2)}, u32[]{:S(2)}) collective-permute-start(bf16[512,256]{1,0:T(8,128)(2,1)S(1)} %collective-permute-done.e1_ref), channel_id=1, source_target_pairs={{0,8},{8,16},{16,24},{12,4},{20,12},{28,20},{1,9},{9,17},{17,25},{... | collective-permute-start | bytes 786440 | tf_op jit(solution)/shard_map/ppermute | solution.py:392
  21.6 0.0 collective-permute-done.1.e1_ref
  21.6 0.0 copy-start.13
  21.6 0.7 collective-permute-start.2
  22.2 4.7 %collective-permute-start.6 = (bf16[512,256]{1,0:T(8,128)(2,1)S(1)}, bf16[512,256]{1,0:T(8,128)(2,1)S(1)}, u32[]{:S(2)}, u32[]{:S(2)}) collective-permute-start(bf16[512,256]{1,0:T(8,128)(2,1)S(1)} %collective-permute-done.1.e1_ref), channel_id=1, source_target_pairs={{0,8},{8,16},{16,24},{12,4},{20,12},{28,20},{1,9},{9,17},{17,25},{... | collective-permute-start | bytes 786440 | tf_op jit(solution)/shard_map/ppermute | solution.py:392
  27.0 0.0 collective-permute-done.5
  27.0 1.1 %fusion = (bf16[512,256]{1,0:T(8,128)(2,1)S(1)}, bf16[512,256]{1,0:T(8,128)(2,1)S(1)}) fusion(bf16[512,512]{1,0:T(8,128)(2,1)} %collective-permute-done.5), kind=kLoop, calls=%fused_computation.12 | loop fusion | bytes 1048576 | tf_op jit(solution)/shard_map/slice | solution.py:444
  28.1 0.0 copy-start.3
  28.1 0.0 copy-start.4
  28.1 0.0 copy-start.10
  28.1 0.0 collective-permute-done.4
  28.2 0.4 collective-permute-done.2.e2_ref
  28.5 0.9 %collective-permute-start.3 = (bf16[512,256]{1,0:T(8,128)(2,1)}, bf16[512,256]{1,0:T(8,128)(2,1)S(1)}, u32[]{:S(2)}, u32[]{:S(2)}) collective-permute-start(bf16[512,256]{1,0:T(8,128)(2,1)} %get-tuple-element.42), channel_id=1, source_target_pairs={{0,4},{4,0},{8,12},{12,8},{16,20},{20,16},{24,28},{28,24},{1,5},{5... | collective-permute-start | bytes 786440 | tf_op jit(solution)/shard_map/ppermute | solution.py:19
  29.4 1.2 %collective-permute-done.7.s3_ref = bf16[512,256]{1,0:T(8,128)(2,1)S(1)} collective-permute-done((bf16[512,256]{1,0:T(8,128)(2,1)S(1)}, bf16[512,256]{1,0:T(8,128)(2,1)S(1)}, u32[]{:S(2)}, u32[]{:S(2)}) %collective-permute-start.7) | collective-permute-done | bytes 262176 | tf_op jit(solution)/shard_map/ppermute | solution.py:392
  30.6 0.0 copy-done.14
  30.6 0.0 copy-done.13
  30.6 0.0 copy-done.4
  30.6 0.0 copy-done.10
  30.7 0.7 copy-done.12
  31.3 0.0 copy-start.11
  31.4 8.4 %filter_grad.2 = (f32[72,256]{1,0:T(8,128)S(1)}, f32[64,1536]{1,0:T(8,128)S(1)}) custom-call(s32[2]{0:T(128)S(1)} %pad_add_fusion.par_ref, bf16[512,256]{1,0:T(8,128)(2,1)S(1)} %get-tuple-element.71.xk_ref, bf16[512,256]{1,0:T(8,128)(2,1)S(1)} %get-tuple-element.78.gk_ref, bf16[512,256]{1,0:T(8,128)(2,1)S(1)} %collective-permute-done.e1_ref, ...), custom_call_target="tpu_custom_call" | custom-call | flops 4000000000 | bytes 8388608 | tf_op jit(solution)/shard_map/filter_grad/pallas_call | solution.py:477
  39.8 2.6 %collective-permute-start.13 = (f32[72,256]{1,0:T(8,128)S(1)}, f32[72,256]{1,0:T(8,128)S(1)}, u32[]{:S(2)}, u32[]{:S(2)}) collective-permute-start(f32[72,256]{1,0:T(8,128)S(1)} %get-tuple-element.54), channel_id=1, source_target_pairs={{0,8},{4,12},{8,0},{12,4},{16,24},{20,28},{24,16},{28,20},{1,9},{5... | collective-permute-start | bytes 221192 | tf_op jit(solution)/shard_map/ppermute | solution.py:19
  42.4 0.0 collective-permute-done.6.s3_ref
  42.4 0.0 collective-permute-done.3.e2_ref
  42.4 9.5 %filter_grad.3 = (f32[72,256]{1,0:T(8,128)S(1)}, f32[64,128]{1,0:T(8,128)S(1)}) custom-call(s32[2]{0:T(128)S(1)} %pad_add_fusion.par_ref, bf16[512,256]{1,0:T(8,128)(2,1)S(1)} %get-tuple-element.72.xk_ref, bf16[512,256]{1,0:T(8,128)(2,1)S(1)} %get-tuple-element.77.gk_ref, bf16[512,256]{1,0:T(8,128)(2,1)S(1)} %collective-permute-done.1.e1_ref, ...), custom_call_target="tpu_custom_call" | custom-call | flops 4000000000 | bytes 8388608 | tf_op jit(solution)/shard_map/filter_grad/pallas_call | solution.py:477
  51.9 0.1 collective-permute-start.16
  52.0 0.0 collective-permute-start.8
  52.0 0.0 collective-permute-done.13
  52.1 1.3 %collective-permute-start.14 = (f32[72,256]{1,0:T(8,128)S(1)}, f32[72,256]{1,0:T(8,128)S(1)}, u32[]{:S(2)}, u32[]{:S(2)}) collective-permute-start(f32[72,256]{1,0:T(8,128)S(1)} %add.62), channel_id=1, source_target_pairs={{0,16},{4,20},{8,24},{12,28},{16,0},{20,4},{24,8},{28,12},{1,17},{... | collective-permute-start | bytes 221192 | tf_op jit(solution)/shard_map/ppermute | solution.py:19
  53.4 4.4 %collective-permute-done.16 = f32[72,256]{1,0:T(8,128)S(1)} collective-permute-done((f32[72,256]{1,0:T(8,128)S(1)}, f32[72,256]{1,0:T(8,128)S(1)}, u32[]{:S(2)}, u32[]{:S(2)}) %collective-permute-start.16) | collective-permute-done | bytes 73760 | tf_op jit(solution)/shard_map/ppermute | solution.py:19
  57.8 0.1 collective-permute-start.17
  57.8 0.0 collective-permute-done.8
  57.9 1.6 %collective-permute-start.9 = (f32[64,128]{1,0:T(8,128)S(1)}, f32[64,128]{1,0:T(8,128)S(1)}, u32[]{:S(2)}, u32[]{:S(2)}) collective-permute-start(f32[64,128]{1,0:T(8,128)S(1)} %add.58), channel_id=1, source_target_pairs={{0,2},{1,3},{2,0},{3,1},{4,6},{5,7},{6,4},{7,5},{8,10},{9,11},{10,... | collective-permute-start | bytes 98312 | tf_op jit(solution)/shard_map/ppermute | solution.py:19
  59.4 2.4 %collective-permute-done.9 = f32[64,128]{1,0:T(8,128)S(1)} collective-permute-done((f32[64,128]{1,0:T(8,128)S(1)}, f32[64,128]{1,0:T(8,128)S(1)}, u32[]{:S(2)}, u32[]{:S(2)}) %collective-permute-start.9) | collective-permute-done | bytes 32800 | tf_op jit(solution)/shard_map/ppermute | solution.py:19
  61.8 0.0 collective-permute-start.10
  61.9 0.0 collective-permute-done.14
  61.9 0.0 copy-start.17
  61.9 2.1 %collective-permute-start.15 = (f32[72,256]{1,0:T(8,128)S(1)}, f32[72,256]{1,0:T(8,128)S(1)}, u32[]{:S(2)}, u32[]{:S(2)}) collective-permute-start(f32[72,256]{1,0:T(8,128)S(1)} %add.63.rest_0_), channel_id=1, source_target_pairs={{0,4},{4,0},{8,12},{12,8},{16,20},{20,16},{24,28},{28,24},{1,5},{5... | collective-permute-start | bytes 221192 | tf_op jit(solution)/shard_map/ppermute | solution.py:19
  64.0 0.0 collective-permute-done.17
  64.0 0.5 collective-permute-start.18
  64.5 1.2 %collective-permute-done.10 = f32[64,128]{1,0:T(8,128)S(1)} collective-permute-done((f32[64,128]{1,0:T(8,128)S(1)}, f32[64,128]{1,0:T(8,128)S(1)}, u32[]{:S(2)}, u32[]{:S(2)}) %collective-permute-start.10) | collective-permute-done | bytes 32800 | tf_op jit(solution)/shard_map/ppermute | solution.py:19
  65.8 2.9 %collective-permute-start.11 = (f32[64,128]{1,0:T(8,128)S(1)}, f32[64,128]{1,0:T(8,128)S(1)}, u32[]{:S(2)}, u32[]{:S(2)}) collective-permute-start(f32[64,128]{1,0:T(8,128)S(1)} %add.60), channel_id=1, source_target_pairs={{0,16},{4,20},{8,24},{12,28},{16,0},{20,4},{24,8},{28,12},{1,17},{... | collective-permute-start | bytes 98312 | tf_op jit(solution)/shard_map/ppermute | solution.py:19
  68.7 2.1 %collective-permute-done.11 = f32[64,128]{1,0:T(8,128)S(1)} collective-permute-done((f32[64,128]{1,0:T(8,128)S(1)}, f32[64,128]{1,0:T(8,128)S(1)}, u32[]{:S(2)}, u32[]{:S(2)}) %collective-permute-start.11) | collective-permute-done | bytes 32800 | tf_op jit(solution)/shard_map/ppermute | solution.py:19
  70.8 0.0 copy-done.18
  70.8 0.3 collective-permute-start.12
  71.1 0.0 collective-permute-done.15.rest_1_
  71.1 3.7 %collective-permute-done.12.far_ref = f32[64,128]{1,0:T(8,128)S(1)} collective-permute-done((f32[64,128]{1,0:T(8,128)S(1)}, f32[64,128]{1,0:T(8,128)S(1)}, u32[]{:S(2)}, u32[]{:S(2)}) %collective-permute-start.12) | collective-permute-done | bytes 32800 | tf_op jit(solution)/shard_map/ppermute | solution.py:19
  74.8 0.0 collective-permute-done.18.rest_3_
  74.8 0.6 copy-done.22
  75.4 0.6 copy-done.21
  76.0 1.9 %finish.1 = (f32[17,64]{1,0:T(8,128)}, f32[1,64]{1,0:T(1,128)}, f32[1,64]{1,0:T(1,128)}, f32[64,64]{1,0:T(8,128)}, f32[1,64]{1,0:T(1,128)}, /*index=5*/f32[1,64]...) custom-call(s32[2]{0:T(128)} %copy-done.2, f32[64,128]{1,0:T(8,128)} %copy-done.19, f32[64,128]{1,0:T(8,128)} %copy-done.22, ...), custom_call_target="tpu_custom_call" | custom-call | tf_op jit(solution)/shard_map/finish/pallas_call | solution.py:508
  (39 shorter events, 0.2 us)
Async XLA Ops:
  1.8 11.9 %collective-permute-start = (bf16[512,256]{1,0:T(8,128)(2,1)S(1)}, bf16[512,256]{1,0:T(8,128)(2,1)S(1)}, u32[]{:S(2)}, u32[]{:S(2)}) collective-permute-start(bf16[512,256]{1,0:T(8,128)(2,1)S(1)} %dynamic-slice_select_fusion.1), channel_id=1, source_target_pairs={{0,4},{4,0},{8,12},{12,8},{16,20},{20,16},{24,28},{28,24},{1,5},{5... | collective-permute-start | bytes 786440 | tf_op jit(solution)/shard_map/ppermute | solution.py:19
  4.8 7.7 %copy-start.15 = (bf16[512,1024]{1,0:T(8,128)(2,1)S(1)}, bf16[512,1024]{1,0:T(8,128)(2,1)}, u32[]{:S(2)}) copy-start(bf16[512,1024]{1,0:T(8,128)(2,1)} %param.13) | copy-start | bytes 3145732
  4.8 7.7 %copy-start.16 = (bf16[512,1024]{1,0:T(8,128)(2,1)S(1)}, bf16[512,1024]{1,0:T(8,128)(2,1)}, u32[]{:S(2)}) copy-start(bf16[512,1024]{1,0:T(8,128)(2,1)} %param.14) | copy-start | bytes 3145732
  7.3 19.6 %collective-permute-start.5 = (bf16[512,512]{1,0:T(8,128)(2,1)}, bf16[512,512]{1,0:T(8,128)(2,1)}, u32[]{:S(2)}, u32[]{:S(2)}) collective-permute-start(bf16[512,512]{1,0:T(8,128)(2,1)} %get-tuple-element.64), channel_id=1, source_target_pairs={{8,16},{12,20},{16,8},{20,12},{9,17},{13,21},{17,9},{21,13},{10,18... | collective-permute-start | bytes 1572872 | tf_op jit(solution)/shard_map/ppermute | solution.py:385
  8.8 19.3 %collective-permute-start.4 = (bf16[512,512]{1,0:T(8,128)(2,1)}, bf16[512,512]{1,0:T(8,128)(2,1)S(1)}, u32[]{:S(2)}, u32[]{:S(2)}) collective-permute-start(bf16[512,512]{1,0:T(8,128)(2,1)} %get-tuple-element.65), channel_id=1, source_target_pairs={{0,8},{4,12},{8,0},{12,4},{16,24},{20,28},{24,16},{28,20},{1,9},{5... | collective-permute-start | bytes 1572872 | tf_op jit(solution)/shard_map/ppermute | solution.py:19
  13.6 7.9 %collective-permute-start.1 = (bf16[512,256]{1,0:T(8,128)(2,1)}, bf16[512,256]{1,0:T(8,128)(2,1)S(1)}, u32[]{:S(2)}, u32[]{:S(2)}) collective-permute-start(bf16[512,256]{1,0:T(8,128)(2,1)} %get-tuple-element.40), channel_id=1, source_target_pairs={{0,4},{4,0},{8,12},{12,8},{16,20},{20,16},{24,28},{28,24},{1,5},{5... | collective-permute-start | bytes 786440 | tf_op jit(solution)/shard_map/ppermute | solution.py:19
  14.2 28.2 %copy-start.2 = (s32[2]{0:T(128)}, s32[2]{0:T(128)S(1)}, u32[]{:S(2)}) copy-start(s32[2]{0:T(128)S(1)} %pad_add_fusion.par_ref) | copy-start | bytes 28
  14.2 16.4 %copy-start.14 = (bf16[2,256,256]{2,1,0:T(8,128)(2,1)S(1)}, bf16[2,256,256]{2,1,0:T(8,128)(2,1)}, u32[]{:S(2)}) copy-start(bf16[2,256,256]{2,1,0:T(8,128)(2,1)} %constant.52.clone.inv_ref) | copy-start | bytes 786436
  19.3 11.3 %collective-permute-start.7 = (bf16[512,256]{1,0:T(8,128)(2,1)S(1)}, bf16[512,256]{1,0:T(8,128)(2,1)S(1)}, u32[]{:S(2)}, u32[]{:S(2)}) collective-permute-start(bf16[512,256]{1,0:T(8,128)(2,1)S(1)} %collective-permute-done.e1_ref), channel_id=1, source_target_pairs={{0,8},{8,16},{16,24},{12,4},{20,12},{28,20},{1,9},{9,17},{17,25},{... | collective-permute-start | bytes 786440 | tf_op jit(solution)/shard_map/ppermute | solution.py:392
  21.6 9.0 %copy-start.13 = (bf16[2,512,512]{2,1,0:T(8,128)(2,1)S(1)}, bf16[2,512,512]{2,1,0:T(8,128)(2,1)}, u32[]{:S(2)}) copy-start(bf16[2,512,512]{2,1,0:T(8,128)(2,1)} %constant.51.clone.fwd_ref) | copy-start | bytes 3145732
  21.6 6.9 %collective-permute-start.2 = (bf16[512,256]{1,0:T(8,128)(2,1)}, bf16[512,256]{1,0:T(8,128)(2,1)S(1)}, u32[]{:S(2)}, u32[]{:S(2)}) collective-permute-start(bf16[512,256]{1,0:T(8,128)(2,1)} %get-tuple-element.41), channel_id=1, source_target_pairs={{0,4},{4,0},{8,12},{12,8},{16,20},{20,16},{24,28},{28,24},{1,5},{5... | collective-permute-start | bytes 786440 | tf_op jit(solution)/shard_map/ppermute | solution.py:19
  22.2 20.1 %collective-permute-start.6 = (bf16[512,256]{1,0:T(8,128)(2,1)S(1)}, bf16[512,256]{1,0:T(8,128)(2,1)S(1)}, u32[]{:S(2)}, u32[]{:S(2)}) collective-permute-start(bf16[512,256]{1,0:T(8,128)(2,1)S(1)} %collective-permute-done.1.e1_ref), channel_id=1, source_target_pairs={{0,8},{8,16},{16,24},{12,4},{20,12},{28,20},{1,9},{9,17},{17,25},{... | collective-permute-start | bytes 786440 | tf_op jit(solution)/shard_map/ppermute | solution.py:392
  28.1 2.6 %copy-start.3 = (bf16[128,1536]{1,0:T(8,128)(2,1)S(1)}, bf16[128,1536]{1,0:T(8,128)(2,1)}, u32[]{:S(2)}) copy-start(bf16[128,1536]{1,0:T(8,128)(2,1)} %get-tuple-element.44.acth_ref) | copy-start | bytes 1179652
  28.1 2.6 %copy-start.4 = (bf16[128,1536]{1,0:T(8,128)(2,1)S(1)}, bf16[128,1536]{1,0:T(8,128)(2,1)}, u32[]{:S(2)}) copy-start(bf16[128,1536]{1,0:T(8,128)(2,1)} %get-tuple-element.45.actl_ref) | copy-start | bytes 1179652
  28.1 2.6 %copy-start.10 = (f32[64,1024]{1,0:T(8,128)S(1)}, f32[64,1024]{1,0:T(8,128)}, u32[]{:S(2)}) copy-start(f32[64,1024]{1,0:T(8,128)} %head_ref.3) | copy-start | bytes 786436
  28.5 13.8 %collective-permute-start.3 = (bf16[512,256]{1,0:T(8,128)(2,1)}, bf16[512,256]{1,0:T(8,128)(2,1)S(1)}, u32[]{:S(2)}, u32[]{:S(2)}) collective-permute-start(bf16[512,256]{1,0:T(8,128)(2,1)} %get-tuple-element.42), channel_id=1, source_target_pairs={{0,4},{4,0},{8,12},{12,8},{16,20},{20,16},{24,28},{28,24},{1,5},{5... | collective-permute-start | bytes 786440 | tf_op jit(solution)/shard_map/ppermute | solution.py:19
  30.6 0.7 copy-start.12
  31.3 11.1 %copy-start = (f32[17,1536]{1,0:T(8,128)S(1)}, f32[17,1536]{1,0:T(8,128)}, u32[]{:S(2)}) copy-start(f32[17,1536]{1,0:T(8,128)} %constant.50.clone.feats_ref.rest_3_) | copy-start | bytes 313348
  31.3 11.1 %copy-start.1 = (f32[64,64]{1,0:T(8,128)S(1)}, f32[64,64]{1,0:T(8,128)}, u32[]{:S(2)}) copy-start(f32[64,64]{1,0:T(8,128)} %rest_1_.1) | copy-start | bytes 49156
  31.3 11.1 %copy-start.5 = (f32[64,1536]{1,0:T(8,128)S(1)}, f32[64,1536]{1,0:T(8,128)}, u32[]{:S(2)}) copy-start(f32[64,1536]{1,0:T(8,128)} %get-tuple-element.48.rest_4_) | copy-start | bytes 1179652
  31.3 11.1 %copy-start.6 = (f32[64,1536]{1,0:T(8,128)S(1)}, f32[64,1536]{1,0:T(8,128)}, u32[]{:S(2)}) copy-start(f32[64,1536]{1,0:T(8,128)} %get-tuple-element.49.rest_5_) | copy-start | bytes 1179652
  31.3 11.1 %copy-start.7 = (f32[64,1536]{1,0:T(8,128)S(1)}, f32[64,1536]{1,0:T(8,128)}, u32[]{:S(2)}) copy-start(f32[64,1536]{1,0:T(8,128)} %get-tuple-element.50.rest_6_) | copy-start | bytes 1179652
  31.3 11.1 %copy-start.8 = (f32[64,1536]{1,0:T(8,128)S(1)}, f32[64,1536]{1,0:T(8,128)}, u32[]{:S(2)}) copy-start(f32[64,1536]{1,0:T(8,128)} %get-tuple-element.51.rest_7_) | copy-start | bytes 1179652
  31.3 11.1 %copy-start.9 = (f32[64,1536]{1,0:T(8,128)S(1)}, f32[64,1536]{1,0:T(8,128)}, u32[]{:S(2)}) copy-start(f32[64,1536]{1,0:T(8,128)} %get-tuple-element.52.rest_8_) | copy-start | bytes 1179652
  31.3 11.1 %copy-start.11 = (f32[64,8]{1,0:T(8,128)S(1)}, f32[64,8]{1,0:T(8,128)}, u32[]{:S(2)}) copy-start(f32[64,8]{1,0:T(8,128)} %get-tuple-element.47.rest_2_) | copy-start | bytes 6148
  39.8 12.3 %collective-permute-start.13 = (f32[72,256]{1,0:T(8,128)S(1)}, f32[72,256]{1,0:T(8,128)S(1)}, u32[]{:S(2)}, u32[]{:S(2)}) collective-permute-start(f32[72,256]{1,0:T(8,128)S(1)} %get-tuple-element.54), channel_id=1, source_target_pairs={{0,8},{4,12},{8,0},{12,4},{16,24},{20,28},{24,16},{28,20},{1,9},{5... | collective-permute-start | bytes 221192 | tf_op jit(solution)/shard_map/ppermute | solution.py:19
  51.9 5.8 %collective-permute-start.16 = (f32[72,256]{1,0:T(8,128)S(1)}, f32[72,256]{1,0:T(8,128)S(1)}, u32[]{:S(2)}, u32[]{:S(2)}) collective-permute-start(f32[72,256]{1,0:T(8,128)S(1)} %get-tuple-element.55), channel_id=1, source_target_pairs={{0,8},{4,12},{8,0},{12,4},{16,24},{20,28},{24,16},{28,20},{1,9},{5... | collective-permute-start | bytes 221192 | tf_op jit(solution)/shard_map/ppermute | solution.py:19
  52.0 5.8 %collective-permute-start.8 = (f32[64,128]{1,0:T(8,128)S(1)}, f32[64,128]{1,0:T(8,128)S(1)}, u32[]{:S(2)}, u32[]{:S(2)}) collective-permute-start(f32[64,128]{1,0:T(8,128)S(1)} %get-tuple-element.53), channel_id=1, source_target_pairs={{0,1},{1,0},{2,3},{3,2},{4,5},{5,4},{6,7},{7,6},{8,9},{9,8},{10,11... | collective-permute-start | bytes 98312 | tf_op jit(solution)/shard_map/ppermute | solution.py:19
  52.1 9.8 %collective-permute-start.14 = (f32[72,256]{1,0:T(8,128)S(1)}, f32[72,256]{1,0:T(8,128)S(1)}, u32[]{:S(2)}, u32[]{:S(2)}) collective-permute-start(f32[72,256]{1,0:T(8,128)S(1)} %add.62), channel_id=1, source_target_pairs={{0,16},{4,20},{8,24},{12,28},{16,0},{20,4},{24,8},{28,12},{1,17},{... | collective-permute-start | bytes 221192 | tf_op jit(solution)/shard_map/ppermute | solution.py:19
  57.8 6.2 %collective-permute-start.17 = (f32[72,256]{1,0:T(8,128)S(1)}, f32[72,256]{1,0:T(8,128)S(1)}, u32[]{:S(2)}, u32[]{:S(2)}) collective-permute-start(f32[72,256]{1,0:T(8,128)S(1)} %add.64), channel_id=1, source_target_pairs={{0,16},{4,20},{8,24},{12,28},{16,0},{20,4},{24,8},{28,12},{1,17},{... | collective-permute-start | bytes 221192 | tf_op jit(solution)/shard_map/ppermute | solution.py:19
  57.9 4.0 %collective-permute-start.9 = (f32[64,128]{1,0:T(8,128)S(1)}, f32[64,128]{1,0:T(8,128)S(1)}, u32[]{:S(2)}, u32[]{:S(2)}) collective-permute-start(f32[64,128]{1,0:T(8,128)S(1)} %add.58), channel_id=1, source_target_pairs={{0,2},{1,3},{2,0},{3,1},{4,6},{5,7},{6,4},{7,5},{8,10},{9,11},{10,... | collective-permute-start | bytes 98312 | tf_op jit(solution)/shard_map/ppermute | solution.py:19
  61.8 3.9 %collective-permute-start.10 = (f32[64,128]{1,0:T(8,128)S(1)}, f32[64,128]{1,0:T(8,128)S(1)}, u32[]{:S(2)}, u32[]{:S(2)}) collective-permute-start(f32[64,128]{1,0:T(8,128)S(1)} %add.59), channel_id=1, source_target_pairs={{0,8},{4,12},{8,0},{12,4},{16,24},{20,28},{24,16},{28,20},{1,9},{5... | collective-permute-start | bytes 98312 | tf_op jit(solution)/shard_map/ppermute | solution.py:19
  61.9 2.1 %copy-start.17 = (f32[72,256]{1,0:T(8,128)}, f32[72,256]{1,0:T(8,128)S(1)}, u32[]{:S(2)}) copy-start(f32[72,256]{1,0:T(8,128)S(1)} %add.63.rest_0_) | copy-start | bytes 221188
  61.9 9.2 %collective-permute-start.15 = (f32[72,256]{1,0:T(8,128)S(1)}, f32[72,256]{1,0:T(8,128)S(1)}, u32[]{:S(2)}, u32[]{:S(2)}) collective-permute-start(f32[72,256]{1,0:T(8,128)S(1)} %add.63.rest_0_), channel_id=1, source_target_pairs={{0,4},{4,0},{8,12},{12,8},{16,20},{20,16},{24,28},{28,24},{1,5},{5... | collective-permute-start | bytes 221192 | tf_op jit(solution)/shard_map/ppermute | solution.py:19
  64.0 6.8 %copy-start.18 = (f32[72,256]{1,0:T(8,128)}, f32[72,256]{1,0:T(8,128)S(1)}, u32[]{:S(2)}) copy-start(f32[72,256]{1,0:T(8,128)S(1)} %add.65.rest_2_) | copy-start | bytes 221188
  64.0 10.8 %collective-permute-start.18 = (f32[72,256]{1,0:T(8,128)S(1)}, f32[72,256]{1,0:T(8,128)S(1)}, u32[]{:S(2)}, u32[]{:S(2)}) collective-permute-start(f32[72,256]{1,0:T(8,128)S(1)} %add.65.rest_2_), channel_id=1, source_target_pairs={{0,4},{4,0},{8,12},{12,8},{16,20},{20,16},{24,28},{28,24},{1,5},{5... | collective-permute-start | bytes 221192 | tf_op jit(solution)/shard_map/ppermute | solution.py:19
  65.8 5.0 %collective-permute-start.11 = (f32[64,128]{1,0:T(8,128)S(1)}, f32[64,128]{1,0:T(8,128)S(1)}, u32[]{:S(2)}, u32[]{:S(2)}) collective-permute-start(f32[64,128]{1,0:T(8,128)S(1)} %add.60), channel_id=1, source_target_pairs={{0,16},{4,20},{8,24},{12,28},{16,0},{20,4},{24,8},{28,12},{1,17},{... | collective-permute-start | bytes 98312 | tf_op jit(solution)/shard_map/ppermute | solution.py:19
  70.8 4.0 %copy-start.19 = (f32[64,128]{1,0:T(8,128)}, f32[64,128]{1,0:T(8,128)S(1)}, u32[]{:S(2)}) copy-start(f32[64,128]{1,0:T(8,128)S(1)} %add.61.net_ref) | copy-start | bytes 98308
  70.8 4.0 %collective-permute-start.12 = (f32[64,128]{1,0:T(8,128)S(1)}, f32[64,128]{1,0:T(8,128)S(1)}, u32[]{:S(2)}, u32[]{:S(2)}) collective-permute-start(f32[64,128]{1,0:T(8,128)S(1)} %add.61.net_ref), channel_id=1, source_target_pairs={{0,4},{4,0},{8,12},{12,8},{16,20},{20,16},{24,28},{28,24},{1,5},{5... | collective-permute-start | bytes 98312 | tf_op jit(solution)/shard_map/ppermute | solution.py:19
  71.1 3.7 %copy-start.20 = (f32[72,256]{1,0:T(8,128)}, f32[72,256]{1,0:T(8,128)S(1)}, u32[]{:S(2)}) copy-start(f32[72,256]{1,0:T(8,128)S(1)} %collective-permute-done.15.rest_1_) | copy-start | bytes 221188
  74.8 0.6 copy-start.22
  75.4 0.6 copy-start.21
where the time goes:
time: 78.2 us; the launch traced here: 77.9 us
  starting transfers between devices  28.5 us (36%)
  Pallas kernels  23.7 us (30%)
  waiting for transfers between devices  15.5 us (20%)
  other arithmetic  4.91 us (6%)
  local copies, waits for them, and re-layouts  4.23 us (5%)
  between operations  1.06 us (1%)
    ppermute x16, starting transfers between devices, swapped(): lax.ppermute(value, axis, [(i, i ^ bit) for i in range(lax.axis_size(axis...  20.1 us
    pallas_call x2, Pallas kernels, work(): pl.pallas_call(functools.partial(main_kernel, size, groups, filter_len, f...  17.9 us
    ppermute x16, waiting for transfers between devices, swapped(): lax.ppermute(value, axis, [(i, i ^ bit) for i in range(lax.axis_size(axis...  14.2 us
    ppermute x2, starting transfers between devices, work(): s3.append(lax.ppermute(e1[c], 'seq', ahead + back))  6.96 us
    pallas_call x1, Pallas kernels, work(): pl.pallas_call(prep_kernel, in_specs=[vmem] * 7, out_specs=[vmem] * 8, ou...  3.96 us
    select_n x1, other arithmetic, work(): zb = lax.ppermute(jnp.where(odd == 0, g_keep, x_keep), 'seq', middle)  2.52 us
    unnamed x46, local copies, waits for them, and re-layouts  1.96 us
    pallas_call x1, Pallas kernels, work(): pl.pallas_call(functools.partial(finish_kernel, feats), in_specs=[pl.Bloc...  1.86 us
  transfers between devices with their start and end apart: 19, of which 7 were waited for; matrix products, arithmetic and copies ran while one was open for 8% of the time, Pallas kernels for 28%

commit v1 on v0

--- a/solution.py
+++ b/solution.py
@@ -12,7 +12,6 @@
 
 BANDS = 8
 SPAN_PARTS = 3
-EXACT = lax.Precision.HIGHEST
 
 
 def swapped(value, axis, bit):
@@ -73,14 +72,18 @@
     )
 
 
-def dot32(left, right, dims=(((1,), (0,)), ((), ()))):
-    return lax.dot_general(
-        left, right, dims, precision=EXACT, preferred_element_type=jnp.float32
-    )
-
-
 def dot16(left, right, dims=(((1,), (0,)), ((), ()))):
     return lax.dot_general(left, right, dims, preferred_element_type=jnp.float32)
+
+
+def dot32(left, right, dims=(((1,), (0,)), ((), ()))):
+    left_high, left_low = split_pair(left)
+    right_high, right_low = split_pair(right)
+    return (
+        dot16(left_high, right_high, dims)
+        + dot16(left_high, right_low, dims)
+        + dot16(left_low, right_high, dims)
+    )
 
 
 NT = (((1,), (1,)), ((), ()))
@@ -120,8 +123,7 @@
     mb_ref,
     mf_ref,
     feats_ref,
-    acth_ref,
-    actl_ref,
+    act_ref,
     pre1_ref,
     act1_ref,
     cos1_ref,
@@ -146,8 +148,8 @@
     cos2_ref[...] = second_cos
     for i, value in enumerate((second_act, second_act * feats_ref[0:1, :])):
         high, low = split_pair(value)
-        acth_ref[i * hidden : (i + 1) * hidden, :] = high
-        actl_ref[i * hidden : (i + 1) * hidden, :] = low
+        act_ref[i * hidden : (i + 1) * hidden, :] = high
+        act_ref[(i + 2) * hidden : (i + 3) * hidden, :] = low
 
 
 def main_kernel(
@@ -157,7 +159,6 @@
     first,
     last,
     chunk,
-    par_ref,
     xk_ref,
     gk_ref,
     e1_ref,
@@ -167,8 +168,7 @@
     s3_ref,
     fwd_ref,
     inv_ref,
-    acth_ref,
-    actl_ref,
+    act_ref,
     head_ref,
     rates_ref,
     *rest,
@@ -177,31 +177,38 @@
     second_in = None if first else rest.pop(0)
     if last:
         net_in, rest = rest[:8], rest[8:]
-        part_ref, net_ref, spec, prod, hold, second_ref = rest
+        part_ref, net_ref, stage, sems, spec, prod, hold, delta, second_ref = rest
     else:
-        part_ref, second_ref, spec, prod, hold = rest
-    par = par_ref[0]
-    width = xk_ref.shape[1]
+        part_ref, second_ref, stage, sems, spec, prod, hold, delta = rest
+    seq = lax.axis_index("seq")
+    par, odd = seq % 2, (seq // 2) % 2
+    width = e1_ref.shape[1]
     hidden = head_ref.shape[0]
     mid = size // 2
-
-    def transform(ref, slot):
-        for i in range(2):
-            block = ref[i * size : (i + 1) * size, :]
-            spec[slot + (i ^ par)] = dot16(fwd_ref[par], jnp.concatenate([block, block], axis=0))
-
     half = head_ref.shape[1] // 2
     here = pl.ds(pl.multiple_of(par * half + chunk * width, width), width)
-
-    transform(xk_ref, (WINDOWED + 4) * (1 - par))
-    transform(gk_ref, (WINDOWED + 4) * par)
     before, beyond = WINDOWED - 2 * par, BEYOND + 2 * par
-    odd = par_ref[1]
-    transform(za_ref, beyond + odd * (before - beyond))
-    transform(zb_ref, before + odd * (beyond - before))
-    transform(e1_ref, WINDOWED + 6)
-    transform(e2_ref, FIXED + 2)
-    transform(s3_ref, WINDOWED + 2)
+    sources = [
+        (xk_ref.at[:, here], (WINDOWED + 4) * (1 - par)),
+        (gk_ref.at[:, here], (WINDOWED + 4) * par),
+        (za_ref, beyond + odd * (before - beyond)),
+        (zb_ref, before + odd * (beyond - before)),
+        (e1_ref, WINDOWED + 6),
+        (e2_ref, FIXED + 2),
+        (s3_ref, WINDOWED + 2),
+    ]
+    copies = [
+        pltpu.make_async_copy(source, stage.at[i], sems.at[i])
+        for i, (source, _) in enumerate(sources)
+    ]
+    for copy in copies:
+        copy.start()
+    for n, (_, slot) in enumerate(sources):
+        copies[n].wait()
+        for i in range(2):
+            block = stage[n, i * size : (i + 1) * size, :]
+            both = dot16(fwd_ref[par], block)
+            spec[slot + (i ^ par)] = both[: 2 * size] + both[2 * size :]
 
     lanes = 128
     rows = 16
@@ -270,27 +277,24 @@
     inner = jnp.exp(-(tap.astype(jnp.float32) / filter_len) * rates)
     head = head_ref[:, here]
     head_high, head_low = split_pair(head)
-    total = jnp.zeros((2 * hidden, width), jnp.float32)
     for m in range(groups):
-        grads = []
+        outer = jnp.exp(-(m * size / filter_len) * rates)
         for q in range(2):
             high = prod[2 * m, q * size : (q + 1) * size, :]
             low = prod[2 * m + 1, q * size : (q + 1) * size, :]
             both = dot16(inv_ref[q], high)
-            grads.append(both[:mid] + both[mid:] + dot16(inv_ref[q, :mid, :], low))
-        outer = jnp.exp(-(m * size / filter_len) * rates)
-        delta = jnp.concatenate(grads, axis=0) * (inner * outer)
-        high, low = split_pair(delta)
-        cols = slice(m * size, (m + 1) * size)
-        total += (
-            dot16(acth_ref[:, cols], high)
-            + dot16(acth_ref[:, cols], low)
-            + dot16(actl_ref[:, cols], high)
-        )
-        second = (
-            dot16(head_high, high, NT) + dot16(head_high, low, NT) + dot16(head_low, high, NT)
-        )
-        second_ref[:, cols] = second if first else second + second_in[:, cols]
+            grad = both[:mid] + both[mid:] + dot16(inv_ref[q, :mid, :], low)
+            high, low = split_pair(grad * (inner[q * mid : (q + 1) * mid] * outer))
+            at = m * size + q * mid
+            delta[0, at : at + mid, :] = high
+            delta[1, at : at + mid, :] = low
+    stacked = dot16(act_ref[...], delta[0])
+    total = (
+        stacked[: 2 * hidden] + stacked[2 * hidden :] + dot16(act_ref[: 2 * hidden, :], delta[1])
+    )
+    stacked = dot16(jnp.concatenate([head_high, head_low], axis=0), delta[0], NT)
+    second = stacked[:hidden] + stacked[hidden:] + dot16(head_high, delta[1], NT)
+    second_ref[...] = second if first else second + second_in[...]
 
     part_ref[:hidden, :] = total[:hidden]
     part_ref[hidden:, :] = jnp.broadcast_to(
@@ -315,10 +319,10 @@
         net_ref[:, at:] = jnp.zeros((hidden, net_ref.shape[1] - at), jnp.float32)
 
 
-def finish_kernel(count, par_ref, net_ref, far_ref, *rest):
+def finish_kernel(count, net_ref, far_ref, *rest):
     ew_ref, eb_ref, ef_ref, mw_ref, mb_ref, mf_ref, head_ref, rates_ref = rest[-8:]
     parts = rest[:-8]
-    par = par_ref[0]
+    par = lax.axis_index("seq") % 2
     turned = (net_ref[...] + far_ref[...]).T
     hidden = turned.shape[1]
     mw_ref[...] = turned[:hidden]
@@ -371,38 +375,43 @@
         return jnp.where(par == 0, g_give, x_give), jnp.where(par == 0, x_give, g_give)
 
     odd = (lax.axis_index("seq") // 2) % 2
-    place = jnp.stack([par, odd]).astype(jnp.int32)
     ahead = [(i, i + 2) for i in range(0, count - 2, 2)]
     back = [(i, i - 2) for i in range(3, count, 2)]
     upper = [i for i in range(count - 2) if (i // 2) % 2 == 1]
     middle = [(i, i + 2) for i in upper] + [(i + 2, i) for i in upper]
-    one0, _ = gives(inputs, out_grad, 0)
-    e1 = [swapped(one0, "seq", 1)]
-    own_in, own_grad, _ = lax.optimization_barrier((inputs, out_grad, one0))
-    x_keep = part_of(own_in, par, 0, half)
-    g_keep = part_of(own_grad, par, 0, half)
-    za = swapped(jnp.where(odd == 0, x_keep, g_keep), "seq", 2)
-    zb = lax.ppermute(jnp.where(odd == 0, g_keep, x_keep), "seq", middle)
-    own_in, own_grad, _ = lax.optimization_barrier((own_in, own_grad, x_keep))
-    sends = [gives(own_in, own_grad, c) for c in chunks]
-    e2, s3 = [], []
-    for c in chunks[1:]:
-        e1.append(swapped(after(sends[c][0], e1[-1]), "seq", 1))
+
+    def halos(x_all, g_all, chunk):
+        x_keep = part_of(x_all, par, chunk, width)
+        g_keep = part_of(g_all, par, chunk, width)
+        return jnp.where(odd == 0, x_keep, g_keep), jnp.where(odd == 0, g_keep, x_keep)
+
+    e1, e2, s3, za, zb = [], [], [], [], []
+    own_in, own_grad = inputs, out_grad
     for c in chunks:
+        one, _ = gives(own_in, own_grad, c)
+        e1.append(swapped(one, "seq", 1))
+        own_in, own_grad, _ = lax.optimization_barrier((own_in, own_grad, one))
+    for c in chunks:
+        up, down = halos(own_in, own_grad, c)
+        za.append(swapped(up, "seq", 2))
+        zb.append(lax.ppermute(down, "seq", middle))
+        own_in, own_grad, _, _ = lax.optimization_barrier((own_in, own_grad, up, down))
+    for c in chunks:
+        _, two = gives(own_in, own_grad, c)
         s3.append(lax.ppermute(e1[c], "seq", ahead + back))
-    for c in chunks:
-        e2.append(swapped(after(sends[c][1], e1[-1] if c == 0 else e2[-1]), "seq", 1))
+        e2.append(swapped(after(two, e1[c]), "seq", 1))
 
     features = jnp.asarray(tap_features(filter_len, size, BANDS))
     feats = features.shape[0]
     taps = jax.ShapeDtypeStruct((hidden, filter_len), jnp.float32)
-    wide = jax.ShapeDtypeStruct((2 * hidden, filter_len), jnp.bfloat16)
+    wide = jax.ShapeDtypeStruct((4 * hidden, filter_len), jnp.bfloat16)
     vmem = pl.BlockSpec(memory_space=pltpu.VMEM)
     made = pl.pallas_call(
         prep_kernel,
         in_specs=[vmem] * 7,
-        out_specs=[vmem] * 8,
-        out_shape=[wide, wide] + [taps] * 5 + [jax.ShapeDtypeStruct((hidden, 8), jnp.float32)],
+        out_specs=[vmem] * 7,
+        out_shape=[wide] + [taps] * 5 + [jax.ShapeDtypeStruct((hidden, 8), jnp.float32)],
+        compiler_params=pltpu.CompilerParams(vmem_limit_bytes=16 * 2**20),
         name="prep",
     )(
         after(embed_weight, e1[0]),
@@ -413,11 +422,11 @@
         mixer_freq[None, :],
         features,
     )
-    act_high, act_low, first_pre, first_act, first_cos, second_pre, second_cos, cols = made
+    act, first_pre, first_act, first_cos, second_pre, second_cos, cols = made
 
     (fwd_high, fwd_low), (inv_high, inv_low) = transforms(size)
-    forward = np.concatenate([fwd_high, fwd_low], axis=1)
-    mirrored = np.concatenate([forward[:size], -forward[size:]], axis=0)
+    forward = np.concatenate([fwd_high, fwd_low], axis=0)
+    mirrored = forward * np.where(np.arange(4 * size) // size % 2, -1, 1)[:, None].astype(forward.dtype)
     forward = jnp.asarray(np.stack([forward, mirrored]))
     mid = size // 2
     inverse = jnp.asarray(
@@ -431,22 +440,20 @@
 
     parts = []
     second_grad = None
+    late_in, late_grad, _ = lax.optimization_barrier((inputs, out_grad, e1[0]))
     for c in chunks:
         first, last = c == 0, c == chunks[-1]
-        here = slice(c * width, (c + 1) * width)
         operands = [
-            place,
-            x_keep[:, here],
-            g_keep[:, here],
+            late_in,
+            late_grad,
             e1[c],
             e2[c],
-            za[:, here],
-            zb[:, here],
+            za[c],
+            zb[c],
             s3[c],
             forward,
             inverse,
-            act_high,
-            act_low,
+            act,
             head_weight,
             decay_rates[None, :],
         ]
@@ -455,9 +462,12 @@
         part_shape = jax.ShapeDtypeStruct((hidden + 8, width), jnp.float32)
         second_shape = jax.ShapeDtypeStruct((hidden, filter_len), jnp.float32)
         scratch = [
+            pltpu.VMEM((7, block_len, width), jnp.bfloat16),
+            pltpu.SemaphoreType.DMA((7,)),
             pltpu.VMEM((14, 2 * size, width), jnp.float32),
             pltpu.VMEM((2 * groups, 2 * size, width), jnp.bfloat16),
             pltpu.VMEM((2 * groups, 16, 128), jnp.float32),
+            pltpu.VMEM((2, filter_len, width), jnp.bfloat16),
         ]
         if last:
             operands += [
@@ -476,8 +486,8 @@
             out_shape = [part_shape, second_shape]
         part, out = pl.pallas_call(
             functools.partial(main_kernel, size, groups, filter_len, first, last, c),
-            in_specs=[pl.BlockSpec(memory_space=pltpu.SMEM)]
-            + [pl.BlockSpec(memory_space=pltpu.VMEM)] * (len(operands) - 1),
+            in_specs=[pl.BlockSpec(memory_space=pltpu.HBM)] * 7
+            + [pl.BlockSpec(memory_space=pltpu.VMEM)] * (len(operands) - 7),
             out_specs=[pl.BlockSpec(memory_space=pltpu.VMEM)] * 2,
             out_shape=out_shape,
             scratch_shapes=scratch,
@@ -507,8 +517,7 @@
     row = jax.ShapeDtypeStruct((1, hidden), jnp.float32)
     outs = pl.pallas_call(
         functools.partial(finish_kernel, feats),
-        in_specs=[pl.BlockSpec(memory_space=pltpu.SMEM)]
-        + [pl.BlockSpec(memory_space=pltpu.VMEM)] * (2 + len(both)),
+        in_specs=[pl.BlockSpec(memory_space=pltpu.VMEM)] * (2 + len(both)),
         out_specs=[pl.BlockSpec(memory_space=pltpu.VMEM)] * 8,
         out_shape=[
             jax.ShapeDtypeStruct((feats, hidden), jnp.float32),
@@ -520,8 +529,9 @@
             jax.ShapeDtypeStruct((hidden, chan_count), jnp.float32),
             jax.ShapeDtypeStruct((1, chan_count), jnp.float32),
         ],
+        compiler_params=pltpu.CompilerParams(vmem_limit_bytes=8 * 2**20),
         name="finish",
-    )(place, net, far, *both)
+    )(net, far, *both)
     return tuple(o[0] if o.shape[0] == 1 else o for o in outs)
 
 

time: 78.2 us -> 74.5 us (0.953)
  Pallas kernels: 23.7 us -> 19.5 us
  local copies, waits for them, and re-layouts: 4.23 us -> 0.71 us
  starting transfers between devices: 28.5 us -> 31.4 us
  other arithmetic: 4.91 us -> 5.93 us
    ppermute x2, starting transfers between devices: 6.96 us -> 11.8 us  [work(): s3.append(lax.ppermute(e1[c], 'seq', ahead + back))]
    select_n x1 -> x2, other arithmetic: 1.1 us -> 3.69 us  [gives(): jnp.where(par == 0, g_give, x_give)]
    slice x3 -> x0, local copies, waits for them, and re-layouts: 2.28 us -> none  [the longest x1 1.18 us: work(): x_keep[:, here]]
    pallas_call x1, Pallas kernels: 3.96 us -> 1.74 us  [work(): pl.pallas_call(prep_kernel, in_specs=[vmem] * 7, out_specs=[vmem] * 7, ou...]
    ppermute x16 -> x17, starting transfers between devices: 20.1 us -> 18.2 us  [swapped(): lax.ppermute(value, axis, [(i, i ^ bit) for i in range(lax.axis_size(axis...]
    ppermute x16 -> x17, waiting for transfers between devices: 14.2 us -> 15.7 us  [swapped(): lax.ppermute(value, axis, [(i, i ^ bit) for i in range(lax.axis_size(axis...]
    unnamed x46 -> x26, local copies, waits for them, and re-layouts: 1.96 us -> 0.71 us
    ppermute x2, waiting for transfers between devices: 1.24 us -> 0.01 us  [work(): s3.append(lax.ppermute(e1[c], 'seq', ahead + back))]
  transfers between devices with their start and end apart: 19 -> 21, of which waited for: 7 -> 7; matrix products, arithmetic and copies ran while one was open for 8% -> 5% of each run, Pallas kernels for 28% -> 13%
where the time goes in v1:
time: 74.5 us; the launch traced here: 74.2 us
  starting transfers between devices  31.4 us (42%)
  Pallas kernels  19.5 us (26%)
  waiting for transfers between devices  15.7 us (21%)
  other arithmetic  5.93 us (8%)
  between operations  0.98 us (1%)
    ppermute x17, starting transfers between devices, swapped(): lax.ppermute(value, axis, [(i, i ^ bit) for i in range(lax.axis_size(axis...  18.2 us
    pallas_call x2, Pallas kernels, work(): pl.pallas_call(functools.partial(main_kernel, size, groups, filter_len, f...  16.9 us
    ppermute x17, waiting for transfers between devices, swapped(): lax.ppermute(value, axis, [(i, i ^ bit) for i in range(lax.axis_size(axis...  15.7 us
    ppermute x2, starting transfers between devices, work(): s3.append(lax.ppermute(e1[c], 'seq', ahead + back))  11.8 us
    select_n x2, other arithmetic, gives(): jnp.where(par == 0, g_give, x_give)  3.69 us
    select_n x2, other arithmetic, halos(): jnp.where(odd == 0, g_keep, x_keep)  1.9 us
    pallas_call x1, Pallas kernels, work(): pl.pallas_call(prep_kernel, in_specs=[vmem] * 7, out_specs=[vmem] * 7, ou...  1.74 us
  transfers between devices with their start and end apart: 21, of which 7 were waited for; matrix products, arithmetic and copies ran while one was open for 5% of the time, Pallas kernels for 13%

profile of v1, /device:TPU:0, one launch (start us, length us, event | category | flops | bytes accessed | tf_op | source)
XLA Modules:
  0.0 74.2 jit_solution(7715981453768052362)
XLA Ops:
  0.6 0.0 copy-start
  0.7 1.9 %dynamic-slice_select_fusion.3 = bf16[512,256]{1,0:T(8,128)(2,1)} fusion(bf16[512,1024]{1,0:T(8,128)(2,1)} %xk_ref.1, s32[]{:T(128)S(6)} %select_n.75, bf16[512,1024]{1,0:T(8,128)(2,1)} %gk_ref.1, pred[]{:T(512)S(6)} %eq.7), kind=kLoop, calls=%fused_computation.3 | loop fusion | flops 131072 | bytes 786437 | tf_op jit(solution)/shard_map/jit(_where)/select_n | solution.py:375
  2.6 3.0 %collective-permute-start = (bf16[512,256]{1,0:T(8,128)(2,1)}, bf16[512,256]{1,0:T(8,128)(2,1)S(1)}, u32[]{:S(2)}, u32[]{:S(2)}) collective-permute-start(bf16[512,256]{1,0:T(8,128)(2,1)} %dynamic-slice_select_fusion.3), channel_id=1, source_target_pairs={{0,4},{4,0},{8,12},{12,8},{16,20},{20,16},{24,28},{28,24},{1,5},{5... | collective-permute-start | bytes 786440 | tf_op jit(solution)/shard_map/ppermute | solution.py:18
  5.6 1.8 %dynamic-slice_select_fusion.2 = bf16[512,256]{1,0:T(8,128)(2,1)} fusion(bf16[512,1024]{1,0:T(8,128)(2,1)} %xk_ref.1, s32[]{:T(128)S(6)} %select_n.77, bf16[512,1024]{1,0:T(8,128)(2,1)} %gk_ref.1, pred[]{:T(512)S(6)} %eq.7), kind=kLoop, calls=%fused_computation.2 | loop fusion | flops 131072 | bytes 786437 | tf_op jit(solution)/shard_map/jit(_where)/select_n | solution.py:375
  7.4 0.1 collective-permute-start.1
  7.5 1.7 %broadcast_select_fusion.2 = (bf16[512,256]{1,0:T(8,128)(2,1)S(1)}, bf16[512,256]{1,0:T(8,128)(2,1)}) fusion(pred[]{:T(512)S(6)} %eq.8, bf16[512,1024]{1,0:T(8,128)(2,1)} %gk_ref.1, s32[]{:T(128)S(6)} %select_n.82, bf16[512,1024]{1,0:T(8,128)(2,1)S(1)} %copy-done), kind=kLoop, calls=%fused_computation.6 | loop fusion | flops 262144 | bytes 1048581 | tf_op jit(solution)/shard_map/jit(_where)/select_n | solution.py:386
  9.2 2.0 %collective-permute-start.7 = (bf16[512,256]{1,0:T(8,128)(2,1)}, bf16[512,256]{1,0:T(8,128)(2,1)S(1)}, u32[]{:S(2)}, u32[]{:S(2)}) collective-permute-start(bf16[512,256]{1,0:T(8,128)(2,1)} %get-tuple-element.77), channel_id=1, source_target_pairs={{0,8},{4,12},{8,0},{12,4},{16,24},{20,28},{24,16},{28,20},{1,9},{5... | collective-permute-start | bytes 786440 | tf_op jit(solution)/shard_map/ppermute | solution.py:18
  11.2 0.7 collective-permute-start.8
  11.9 0.0 copy-done.1
  11.9 0.0 copy-start.12
  11.9 0.2 broadcast_select_fusion
  12.1 0.0 copy-start.11
  12.1 0.0 copy-start.2
  12.1 0.0 copy-start.3
  12.1 0.0 copy-start.4
  12.1 0.0 copy-start.8
  12.1 0.0 copy-start.9
  12.1 0.3 dynamic-slice_select_fusion
  12.4 0.5 collective-permute-done.e1_ref
  12.9 2.0 %collective-permute-start.6 = (bf16[512,256]{1,0:T(8,128)(2,1)S(1)}, bf16[512,256]{1,0:T(8,128)(2,1)S(1)}, u32[]{:S(2)}, u32[]{:S(2)}) collective-permute-start(bf16[512,256]{1,0:T(8,128)(2,1)S(1)} %get-tuple-element.53), channel_id=1, source_target_pairs={{0,4},{4,0},{8,12},{12,8},{16,20},{20,16},{24,28},{28,24},{1,5},{5... | collective-permute-start | bytes 786440 | tf_op jit(solution)/shard_map/ppermute | solution.py:18
  14.9 5.4 %collective-permute-start.9 = (bf16[512,256]{1,0:T(8,128)(2,1)S(1)}, bf16[512,256]{1,0:T(8,128)(2,1)S(1)}, u32[]{:S(2)}, u32[]{:S(2)}) collective-permute-start(bf16[512,256]{1,0:T(8,128)(2,1)S(1)} %collective-permute-done.e1_ref), channel_id=1, source_target_pairs={{0,8},{8,16},{16,24},{12,4},{20,12},{28,20},{1,9},{9,17},{17,25},{... | collective-permute-start | bytes 786440 | tf_op jit(solution)/shard_map/ppermute | solution.py:401
  20.3 0.0 collective-permute-done.1.e1_ref
  20.3 0.3 collective-permute-start.3
  20.7 0.6 copy-done.5
  21.3 0.0 copy-done.6
  21.3 0.0 copy-done.7
  21.3 1.7 %prep.1 = (bf16[256,1536]{1,0:T(8,128)(2,1)S(1)}, f32[64,1536]{1,0:T(8,128)S(1)}, f32[64,1536]{1,0:T(8,128)S(1)}, f32[64,1536]{1,0:T(8,128)S(1)}, f32[64,1536]{1...) custom-call(f32[17,64]{1,0:T(8,128)S(1)} %copy-done.4, f32[1,64]{1,0:T(1,128)S(1)} %bitcast.10, ...), custom_call_target="tpu_custom_call" | custom-call | tf_op jit(solution)/shard_map/prep/pallas_call | solution.py:409
  23.1 0.0 collective-permute-done.7.za_ref
  23.1 0.7 collective-permute-start.4
  23.8 0.0 collective-permute-done.8.zb_ref
  23.8 1.6 %collective-permute-start.2 = (bf16[512,256]{1,0:T(8,128)(2,1)S(1)}, bf16[512,256]{1,0:T(8,128)(2,1)S(1)}, u32[]{:S(2)}, u32[]{:S(2)}) collective-permute-start(bf16[512,256]{1,0:T(8,128)(2,1)S(1)} %get-tuple-element.50), channel_id=1, source_target_pairs={{0,4},{4,0},{8,12},{12,8},{16,20},{20,16},{24,28},{28,24},{1,5},{5... | collective-permute-start | bytes 786440 | tf_op jit(solution)/shard_map/ppermute | solution.py:18
  25.3 0.0 collective-permute-done.6.e2_ref
  25.4 6.5 %collective-permute-start.5 = (bf16[512,256]{1,0:T(8,128)(2,1)S(1)}, bf16[512,256]{1,0:T(8,128)(2,1)S(1)}, u32[]{:S(2)}, u32[]{:S(2)}) collective-permute-start(bf16[512,256]{1,0:T(8,128)(2,1)S(1)} %collective-permute-done.1.e1_ref), channel_id=1, source_target_pairs={{0,8},{8,16},{16,24},{12,4},{20,12},{28,20},{1,9},{9,17},{17,25},{... | collective-permute-start | bytes 786440 | tf_op jit(solution)/shard_map/ppermute | solution.py:401
  31.8 0.0 collective-permute-done.9.s3_ref
  31.9 0.0 copy-done.12
  31.9 8.1 %filter_grad.2 = (f32[72,256]{1,0:T(8,128)S(1)}, f32[64,1536]{1,0:T(8,128)S(1)}) custom-call(bf16[512,1024]{1,0:T(8,128)(2,1)S(1)} %copy-done, bf16[512,1024]{1,0:T(8,128)(2,1)S(1)} %copy-done.1, bf16[512,256]{1,0:T(8,128)(2,1)S(1)} %collective-permute-done.e1_ref, bf16[512,256]{1,0:T(8,128)(2,1)S(1)} %collective-permute-done.6.e2_ref, ...), custom_call_target="tpu_custom_call" | custom-call | flops 4000000000 | bytes 8388608 | tf_op jit(solution)/shard_map/filter_grad/pallas_call | solution.py:487
  40.0 0.0 collective-permute-done.3.za_ref
  40.0 0.0 collective-permute-done.4.zb_ref
  40.0 0.0 collective-permute-done.2.e2_ref
  40.0 0.0 collective-permute-done.5.s3_ref
  40.0 8.9 %filter_grad.3 = (f32[72,256]{1,0:T(8,128)S(1)}, f32[64,128]{1,0:T(8,128)S(1)}) custom-call(bf16[512,1024]{1,0:T(8,128)(2,1)S(1)} %copy-done, bf16[512,1024]{1,0:T(8,128)(2,1)S(1)} %copy-done.1, bf16[512,256]{1,0:T(8,128)(2,1)S(1)} %collective-permute-done.1.e1_ref, bf16[512,256]{1,0:T(8,128)(2,1)S(1)} %collective-permute-done.2.e2_ref, ...), custom_call_target="tpu_custom_call" | custom-call | flops 4000000000 | bytes 8388608 | tf_op jit(solution)/shard_map/filter_grad/pallas_call | solution.py:487
  48.9 0.1 collective-permute-start.18
  49.0 2.0 %collective-permute-start.15 = (f32[72,256]{1,0:T(8,128)S(1)}, f32[72,256]{1,0:T(8,128)S(1)}, u32[]{:S(2)}, u32[]{:S(2)}) collective-permute-start(f32[72,256]{1,0:T(8,128)S(1)} %get-tuple-element.62), channel_id=1, source_target_pairs={{0,8},{4,12},{8,0},{12,4},{16,24},{20,28},{24,16},{28,20},{1,9},{5... | collective-permute-start | bytes 221192 | tf_op jit(solution)/shard_map/ppermute | solution.py:18
  51.0 0.0 collective-permute-start.10
  51.0 2.3 %collective-permute-done.18 = f32[72,256]{1,0:T(8,128)S(1)} collective-permute-done((f32[72,256]{1,0:T(8,128)S(1)}, f32[72,256]{1,0:T(8,128)S(1)}, u32[]{:S(2)}, u32[]{:S(2)}) %collective-permute-start.18) | collective-permute-done | bytes 73760 | tf_op jit(solution)/shard_map/ppermute | solution.py:18
  53.3 0.1 collective-permute-start.19
  53.4 0.7 collective-permute-done.15
  54.1 2.3 %collective-permute-start.16 = (f32[72,256]{1,0:T(8,128)S(1)}, f32[72,256]{1,0:T(8,128)S(1)}, u32[]{:S(2)}, u32[]{:S(2)}) collective-permute-start(f32[72,256]{1,0:T(8,128)S(1)} %add.78), channel_id=1, source_target_pairs={{0,16},{4,20},{8,24},{12,28},{16,0},{20,4},{24,8},{28,12},{1,17},{... | collective-permute-start | bytes 221192 | tf_op jit(solution)/shard_map/ppermute | solution.py:18
  56.4 0.0 collective-permute-done.10
  56.4 1.5 %collective-permute-start.11 = (f32[64,128]{1,0:T(8,128)S(1)}, f32[64,128]{1,0:T(8,128)S(1)}, u32[]{:S(2)}, u32[]{:S(2)}) collective-permute-start(f32[64,128]{1,0:T(8,128)S(1)} %add.74), channel_id=1, source_target_pairs={{0,2},{1,3},{2,0},{3,1},{4,6},{5,7},{6,4},{7,5},{8,10},{9,11},{10,... | collective-permute-start | bytes 98312 | tf_op jit(solution)/shard_map/ppermute | solution.py:18
  58.0 2.4 %collective-permute-done.11 = f32[64,128]{1,0:T(8,128)S(1)} collective-permute-done((f32[64,128]{1,0:T(8,128)S(1)}, f32[64,128]{1,0:T(8,128)S(1)}, u32[]{:S(2)}, u32[]{:S(2)}) %collective-permute-start.11) | collective-permute-done | bytes 32800 | tf_op jit(solution)/shard_map/ppermute | solution.py:18
  60.4 0.0 collective-permute-start.12
  60.4 0.0 collective-permute-done.19
  60.4 1.0 %collective-permute-start.20 = (f32[72,256]{1,0:T(8,128)S(1)}, f32[72,256]{1,0:T(8,128)S(1)}, u32[]{:S(2)}, u32[]{:S(2)}) collective-permute-start(f32[72,256]{1,0:T(8,128)S(1)} %add.81.rest_2_), channel_id=1, source_target_pairs={{0,4},{4,0},{8,12},{12,8},{16,20},{20,16},{24,28},{28,24},{1,5},{5... | collective-permute-start | bytes 221192 | tf_op jit(solution)/shard_map/ppermute | solution.py:18
  61.5 0.0 collective-permute-done.16
  61.5 1.1 %collective-permute-start.17 = (f32[72,256]{1,0:T(8,128)S(1)}, f32[72,256]{1,0:T(8,128)S(1)}, u32[]{:S(2)}, u32[]{:S(2)}) collective-permute-start(f32[72,256]{1,0:T(8,128)S(1)} %add.79.rest_0_), channel_id=1, source_target_pairs={{0,4},{4,0},{8,12},{12,8},{16,20},{20,16},{24,28},{28,24},{1,5},{5... | collective-permute-start | bytes 221192 | tf_op jit(solution)/shard_map/ppermute | solution.py:18
  62.6 2.1 %collective-permute-done.12 = f32[64,128]{1,0:T(8,128)S(1)} collective-permute-done((f32[64,128]{1,0:T(8,128)S(1)}, f32[64,128]{1,0:T(8,128)S(1)}, u32[]{:S(2)}, u32[]{:S(2)}) %collective-permute-start.12) | collective-permute-done | bytes 32800 | tf_op jit(solution)/shard_map/ppermute | solution.py:18
  64.7 0.6 collective-permute-start.13
  65.3 4.2 %collective-permute-done.13 = f32[64,128]{1,0:T(8,128)S(1)} collective-permute-done((f32[64,128]{1,0:T(8,128)S(1)}, f32[64,128]{1,0:T(8,128)S(1)}, u32[]{:S(2)}, u32[]{:S(2)}) %collective-permute-start.13) | collective-permute-done | bytes 32800 | tf_op jit(solution)/shard_map/ppermute | solution.py:18
  69.5 0.4 collective-permute-start.14
  69.9 3.5 %collective-permute-done.14.far_ref = f32[64,128]{1,0:T(8,128)S(1)} collective-permute-done((f32[64,128]{1,0:T(8,128)S(1)}, f32[64,128]{1,0:T(8,128)S(1)}, u32[]{:S(2)}, u32[]{:S(2)}) %collective-permute-start.14) | collective-permute-done | bytes 32800 | tf_op jit(solution)/shard_map/ppermute | solution.py:18
  73.4 0.0 collective-permute-done.20.rest_3_
  73.4 0.0 collective-permute-done.17.rest_1_
  73.4 0.8 %finish.1 = (f32[17,64]{1,0:T(8,128)}, f32[1,64]{1,0:T(1,128)}, f32[1,64]{1,0:T(1,128)}, f32[64,64]{1,0:T(8,128)}, f32[1,64]{1,0:T(1,128)}, /*index=5*/f32[1,64]...) custom-call(f32[64,128]{1,0:T(8,128)S(1)} %add.77.net_ref, f32[64,128]{1,0:T(8,128)S(1)} %collective-permute-done.14.far_ref, ...), custom_call_target="tpu_custom_call" | custom-call | tf_op jit(solution)/shard_map/finish/pallas_call | solution.py:518
  (21 shorter events, 0.1 us)
Async XLA Ops:
  0.6 6.8 %copy-start = (bf16[512,1024]{1,0:T(8,128)(2,1)S(1)}, bf16[512,1024]{1,0:T(8,128)(2,1)}, u32[]{:S(2)}) copy-start(bf16[512,1024]{1,0:T(8,128)(2,1)} %xk_ref.1) | copy-start | bytes 3145732
  2.6 9.3 %copy-start.1 = (bf16[512,1024]{1,0:T(8,128)(2,1)S(1)}, bf16[512,1024]{1,0:T(8,128)(2,1)}, u32[]{:S(2)}) copy-start(bf16[512,1024]{1,0:T(8,128)(2,1)} %gk_ref.1) | copy-start | bytes 3145732
  2.6 10.4 %collective-permute-start = (bf16[512,256]{1,0:T(8,128)(2,1)}, bf16[512,256]{1,0:T(8,128)(2,1)S(1)}, u32[]{:S(2)}, u32[]{:S(2)}) collective-permute-start(bf16[512,256]{1,0:T(8,128)(2,1)} %dynamic-slice_select_fusion.3), channel_id=1, source_target_pairs={{0,4},{4,0},{8,12},{12,8},{16,20},{20,16},{24,28},{28,24},{1,5},{5... | collective-permute-start | bytes 786440 | tf_op jit(solution)/shard_map/ppermute | solution.py:18
  7.4 13.0 %collective-permute-start.1 = (bf16[512,256]{1,0:T(8,128)(2,1)}, bf16[512,256]{1,0:T(8,128)(2,1)S(1)}, u32[]{:S(2)}, u32[]{:S(2)}) collective-permute-start(bf16[512,256]{1,0:T(8,128)(2,1)} %dynamic-slice_select_fusion.2), channel_id=1, source_target_pairs={{0,4},{4,0},{8,12},{12,8},{16,20},{20,16},{24,28},{28,24},{1,5},{5... | collective-permute-start | bytes 786440 | tf_op jit(solution)/shard_map/ppermute | solution.py:18
  9.2 13.9 %collective-permute-start.7 = (bf16[512,256]{1,0:T(8,128)(2,1)}, bf16[512,256]{1,0:T(8,128)(2,1)S(1)}, u32[]{:S(2)}, u32[]{:S(2)}) collective-permute-start(bf16[512,256]{1,0:T(8,128)(2,1)} %get-tuple-element.77), channel_id=1, source_target_pairs={{0,8},{4,12},{8,0},{12,4},{16,24},{20,28},{24,16},{28,20},{1,9},{5... | collective-permute-start | bytes 786440 | tf_op jit(solution)/shard_map/ppermute | solution.py:18
  11.2 12.6 %collective-permute-start.8 = (bf16[512,256]{1,0:T(8,128)(2,1)S(1)}, bf16[512,256]{1,0:T(8,128)(2,1)S(1)}, u32[]{:S(2)}, u32[]{:S(2)}) collective-permute-start(bf16[512,256]{1,0:T(8,128)(2,1)S(1)} %get-tuple-element.76), channel_id=1, source_target_pairs={{8,16},{12,20},{16,8},{20,12},{9,17},{13,21},{17,9},{21,13},{10,18... | collective-permute-start | bytes 786440 | tf_op jit(solution)/shard_map/ppermute | solution.py:397
  11.9 20.0 %copy-start.12 = (bf16[2,256,256]{2,1,0:T(8,128)(2,1)S(1)}, bf16[2,256,256]{2,1,0:T(8,128)(2,1)}, u32[]{:S(2)}) copy-start(bf16[2,256,256]{2,1,0:T(8,128)(2,1)} %constant.53.clone.inv_ref) | copy-start | bytes 786436
  12.1 19.8 %copy-start.11 = (bf16[2,1024,256]{2,1,0:T(8,128)(2,1)S(1)}, bf16[2,1024,256]{2,1,0:T(8,128)(2,1)}, u32[]{:S(2)}) copy-start(bf16[2,1024,256]{2,1,0:T(8,128)(2,1)} %constant.52.clone.fwd_ref) | copy-start | bytes 3145732
  12.1 8.6 %copy-start.2 = (f32[17,1536]{1,0:T(8,128)S(1)}, f32[17,1536]{1,0:T(8,128)}, u32[]{:S(2)}) copy-start(f32[17,1536]{1,0:T(8,128)} %constant.51.clone.feats_ref.rest_3_) | copy-start | bytes 313348
  12.1 8.6 %copy-start.3 = (f32[64,64]{1,0:T(8,128)S(1)}, f32[64,64]{1,0:T(8,128)}, u32[]{:S(2)}) copy-start(f32[64,64]{1,0:T(8,128)} %rest_1_.1) | copy-start | bytes 49156
  12.1 8.6 %copy-start.4 = (f32[17,64]{1,0:T(8,128)S(1)}, f32[17,64]{1,0:T(8,128)}, u32[]{:S(2)}) copy-start(f32[17,64]{1,0:T(8,128)} %ew_ref) | copy-start | bytes 13060
  12.1 8.6 %copy-start.8 = (f32[64]{0:T(128)S(1)}, f32[64]{0:T(128)}, u32[]{:S(2)}) copy-start(f32[64]{0:T(128)} %param.20) | copy-start | bytes 772
  12.1 19.8 %copy-start.9 = (f32[64,1024]{1,0:T(8,128)S(1)}, f32[64,1024]{1,0:T(8,128)}, u32[]{:S(2)}) copy-start(f32[64,1024]{1,0:T(8,128)} %head_ref.3) | copy-start | bytes 786436
  12.9 12.4 %collective-permute-start.6 = (bf16[512,256]{1,0:T(8,128)(2,1)S(1)}, bf16[512,256]{1,0:T(8,128)(2,1)S(1)}, u32[]{:S(2)}, u32[]{:S(2)}) collective-permute-start(bf16[512,256]{1,0:T(8,128)(2,1)S(1)} %get-tuple-element.53), channel_id=1, source_target_pairs={{0,4},{4,0},{8,12},{12,8},{16,20},{20,16},{24,28},{28,24},{1,5},{5... | collective-permute-start | bytes 786440 | tf_op jit(solution)/shard_map/ppermute | solution.py:18
  14.9 16.9 %collective-permute-start.9 = (bf16[512,256]{1,0:T(8,128)(2,1)S(1)}, bf16[512,256]{1,0:T(8,128)(2,1)S(1)}, u32[]{:S(2)}, u32[]{:S(2)}) collective-permute-start(bf16[512,256]{1,0:T(8,128)(2,1)S(1)} %collective-permute-done.e1_ref), channel_id=1, source_target_pairs={{0,8},{8,16},{16,24},{12,4},{20,12},{28,20},{1,9},{9,17},{17,25},{... | collective-permute-start | bytes 786440 | tf_op jit(solution)/shard_map/ppermute | solution.py:401
  20.3 19.7 %collective-permute-start.3 = (bf16[512,256]{1,0:T(8,128)(2,1)S(1)}, bf16[512,256]{1,0:T(8,128)(2,1)S(1)}, u32[]{:S(2)}, u32[]{:S(2)}) collective-permute-start(bf16[512,256]{1,0:T(8,128)(2,1)S(1)} %get-tuple-element.75), channel_id=1, source_target_pairs={{0,8},{4,12},{8,0},{12,4},{16,24},{20,28},{24,16},{28,20},{1,9},{5... | collective-permute-start | bytes 786440 | tf_op jit(solution)/shard_map/ppermute | solution.py:18
  20.6 0.7 copy-start.5
  20.6 0.7 copy-start.6
  20.6 0.7 copy-start.7
  21.3 10.6 %copy-start.10 = (f32[1024]{0:T(1024)S(1)}, f32[1024]{0:T(1024)}, u32[]{:S(2)}) copy-start(f32[1024]{0:T(1024)} %param.22) | copy-start | bytes 12292
  23.1 16.9 %collective-permute-start.4 = (bf16[512,256]{1,0:T(8,128)(2,1)S(1)}, bf16[512,256]{1,0:T(8,128)(2,1)S(1)}, u32[]{:S(2)}, u32[]{:S(2)}) collective-permute-start(bf16[512,256]{1,0:T(8,128)(2,1)S(1)} %get-tuple-element.74), channel_id=1, source_target_pairs={{8,16},{12,20},{16,8},{20,12},{9,17},{13,21},{17,9},{21,13},{10,18... | collective-permute-start | bytes 786440 | tf_op jit(solution)/shard_map/ppermute | solution.py:397
  23.8 16.2 %collective-permute-start.2 = (bf16[512,256]{1,0:T(8,128)(2,1)S(1)}, bf16[512,256]{1,0:T(8,128)(2,1)S(1)}, u32[]{:S(2)}, u32[]{:S(2)}) collective-permute-start(bf16[512,256]{1,0:T(8,128)(2,1)S(1)} %get-tuple-element.50), channel_id=1, source_target_pairs={{0,4},{4,0},{8,12},{12,8},{16,20},{20,16},{24,28},{28,24},{1,5},{5... | collective-permute-start | bytes 786440 | tf_op jit(solution)/shard_map/ppermute | solution.py:18
  25.4 14.7 %collective-permute-start.5 = (bf16[512,256]{1,0:T(8,128)(2,1)S(1)}, bf16[512,256]{1,0:T(8,128)(2,1)S(1)}, u32[]{:S(2)}, u32[]{:S(2)}) collective-permute-start(bf16[512,256]{1,0:T(8,128)(2,1)S(1)} %collective-permute-done.1.e1_ref), channel_id=1, source_target_pairs={{0,8},{8,16},{16,24},{12,4},{20,12},{28,20},{1,9},{9,17},{17,25},{... | collective-permute-start | bytes 786440 | tf_op jit(solution)/shard_map/ppermute | solution.py:401
  48.9 4.4 %collective-permute-start.18 = (f32[72,256]{1,0:T(8,128)S(1)}, f32[72,256]{1,0:T(8,128)S(1)}, u32[]{:S(2)}, u32[]{:S(2)}) collective-permute-start(f32[72,256]{1,0:T(8,128)S(1)} %get-tuple-element.63), channel_id=1, source_target_pairs={{0,8},{4,12},{8,0},{12,4},{16,24},{20,28},{24,16},{28,20},{1,9},{5... | collective-permute-start | bytes 221192 | tf_op jit(solution)/shard_map/ppermute | solution.py:18
  49.0 5.1 %collective-permute-start.15 = (f32[72,256]{1,0:T(8,128)S(1)}, f32[72,256]{1,0:T(8,128)S(1)}, u32[]{:S(2)}, u32[]{:S(2)}) collective-permute-start(f32[72,256]{1,0:T(8,128)S(1)} %get-tuple-element.62), channel_id=1, source_target_pairs={{0,8},{4,12},{8,0},{12,4},{16,24},{20,28},{24,16},{28,20},{1,9},{5... | collective-permute-start | bytes 221192 | tf_op jit(solution)/shard_map/ppermute | solution.py:18
  51.0 5.4 %collective-permute-start.10 = (f32[64,128]{1,0:T(8,128)S(1)}, f32[64,128]{1,0:T(8,128)S(1)}, u32[]{:S(2)}, u32[]{:S(2)}) collective-permute-start(f32[64,128]{1,0:T(8,128)S(1)} %get-tuple-element.61), channel_id=1, source_target_pairs={{0,1},{1,0},{2,3},{3,2},{4,5},{5,4},{6,7},{7,6},{8,9},{9,8},{10,11... | collective-permute-start | bytes 98312 | tf_op jit(solution)/shard_map/ppermute | solution.py:18
  53.3 7.1 %collective-permute-start.19 = (f32[72,256]{1,0:T(8,128)S(1)}, f32[72,256]{1,0:T(8,128)S(1)}, u32[]{:S(2)}, u32[]{:S(2)}) collective-permute-start(f32[72,256]{1,0:T(8,128)S(1)} %add.80), channel_id=1, source_target_pairs={{0,16},{4,20},{8,24},{12,28},{16,0},{20,4},{24,8},{28,12},{1,17},{... | collective-permute-start | bytes 221192 | tf_op jit(solution)/shard_map/ppermute | solution.py:18
  54.1 7.3 %collective-permute-start.16 = (f32[72,256]{1,0:T(8,128)S(1)}, f32[72,256]{1,0:T(8,128)S(1)}, u32[]{:S(2)}, u32[]{:S(2)}) collective-permute-start(f32[72,256]{1,0:T(8,128)S(1)} %add.78), channel_id=1, source_target_pairs={{0,16},{4,20},{8,24},{12,28},{16,0},{20,4},{24,8},{28,12},{1,17},{... | collective-permute-start | bytes 221192 | tf_op jit(solution)/shard_map/ppermute | solution.py:18
  56.4 4.0 %collective-permute-start.11 = (f32[64,128]{1,0:T(8,128)S(1)}, f32[64,128]{1,0:T(8,128)S(1)}, u32[]{:S(2)}, u32[]{:S(2)}) collective-permute-start(f32[64,128]{1,0:T(8,128)S(1)} %add.74), channel_id=1, source_target_pairs={{0,2},{1,3},{2,0},{3,1},{4,6},{5,7},{6,4},{7,5},{8,10},{9,11},{10,... | collective-permute-start | bytes 98312 | tf_op jit(solution)/shard_map/ppermute | solution.py:18
  60.4 4.3 %collective-permute-start.12 = (f32[64,128]{1,0:T(8,128)S(1)}, f32[64,128]{1,0:T(8,128)S(1)}, u32[]{:S(2)}, u32[]{:S(2)}) collective-permute-start(f32[64,128]{1,0:T(8,128)S(1)} %add.75), channel_id=1, source_target_pairs={{0,8},{4,12},{8,0},{12,4},{16,24},{20,28},{24,16},{28,20},{1,9},{5... | collective-permute-start | bytes 98312 | tf_op jit(solution)/shard_map/ppermute | solution.py:18
  60.4 13.0 %collective-permute-start.20 = (f32[72,256]{1,0:T(8,128)S(1)}, f32[72,256]{1,0:T(8,128)S(1)}, u32[]{:S(2)}, u32[]{:S(2)}) collective-permute-start(f32[72,256]{1,0:T(8,128)S(1)} %add.81.rest_2_), channel_id=1, source_target_pairs={{0,4},{4,0},{8,12},{12,8},{16,20},{20,16},{24,28},{28,24},{1,5},{5... | collective-permute-start | bytes 221192 | tf_op jit(solution)/shard_map/ppermute | solution.py:18
  61.5 11.9 %collective-permute-start.17 = (f32[72,256]{1,0:T(8,128)S(1)}, f32[72,256]{1,0:T(8,128)S(1)}, u32[]{:S(2)}, u32[]{:S(2)}) collective-permute-start(f32[72,256]{1,0:T(8,128)S(1)} %add.79.rest_0_), channel_id=1, source_target_pairs={{0,4},{4,0},{8,12},{12,8},{16,20},{20,16},{24,28},{28,24},{1,5},{5... | collective-permute-start | bytes 221192 | tf_op jit(solution)/shard_map/ppermute | solution.py:18
  64.7 4.8 %collective-permute-start.13 = (f32[64,128]{1,0:T(8,128)S(1)}, f32[64,128]{1,0:T(8,128)S(1)}, u32[]{:S(2)}, u32[]{:S(2)}) collective-permute-start(f32[64,128]{1,0:T(8,128)S(1)} %add.76), channel_id=1, source_target_pairs={{0,16},{4,20},{8,24},{12,28},{16,0},{20,4},{24,8},{28,12},{1,17},{... | collective-permute-start | bytes 98312 | tf_op jit(solution)/shard_map/ppermute | solution.py:18
  69.5 3.9 %collective-permute-start.14 = (f32[64,128]{1,0:T(8,128)S(1)}, f32[64,128]{1,0:T(8,128)S(1)}, u32[]{:S(2)}, u32[]{:S(2)}) collective-permute-start(f32[64,128]{1,0:T(8,128)S(1)} %add.77.net_ref), channel_id=1, source_target_pairs={{0,4},{4,0},{8,12},{12,8},{16,20},{20,16},{24,28},{28,24},{1,5},{5... | collective-permute-start | bytes 98312 | tf_op jit(solution)/shard_map/ppermute | solution.py:18

commit v2 on v1

--- a/solution.py
+++ b/solution.py
@@ -365,14 +365,14 @@
     width = min(256, half)
     chunks = range(half // width)
 
-    def part_of(value, which, chunk, span):
-        start = which * half + chunk * span
-        return lax.dynamic_slice_in_dim(value, start, span, axis=1)
-
-    def gives(inputs, out_grad, chunk):
-        x_give = part_of(inputs, 1 - par, chunk, width)
-        g_give = part_of(out_grad, 1 - par, chunk, width)
-        return jnp.where(par == 0, g_give, x_give), jnp.where(par == 0, x_give, g_give)
+    def columns(value, which, chunk):
+        start = which * half + chunk * width
+        return value[:, start : start + width]
+
+    def gives(x_all, g_all, chunk):
+        one = jnp.where(par == 0, columns(g_all, 1, chunk), columns(x_all, 0, chunk))
+        two = jnp.where(par == 0, columns(x_all, 1, chunk), columns(g_all, 0, chunk))
+        return one, two
 
     odd = (lax.axis_index("seq") // 2) % 2
     ahead = [(i, i + 2) for i in range(0, count - 2, 2)]
@@ -381,8 +381,8 @@
     middle = [(i, i + 2) for i in upper] + [(i + 2, i) for i in upper]
 
     def halos(x_all, g_all, chunk):
-        x_keep = part_of(x_all, par, chunk, width)
-        g_keep = part_of(g_all, par, chunk, width)
+        x_keep = jnp.where(par == 0, columns(x_all, 0, chunk), columns(x_all, 1, chunk))
+        g_keep = jnp.where(par == 0, columns(g_all, 0, chunk), columns(g_all, 1, chunk))
         return jnp.where(odd == 0, x_keep, g_keep), jnp.where(odd == 0, g_keep, x_keep)
 
     e1, e2, s3, za, zb = [], [], [], [], []

time: 74.5 us -> 73.5 us (0.987)
  other arithmetic: 5.93 us -> 3.5 us
  waiting for transfers between devices: 15.7 us -> 17.3 us
    select_n x3, other arithmetic: 3.96 us -> 2.27 us  [the longest x2 2.21 us: gives(): jnp.where(par == 0, columns(g_all, 1, chunk), columns(x_all, 0, chunk))]
    ppermute x2, starting transfers between devices: 11.8 us -> 10.3 us  [work(): s3.append(lax.ppermute(e1[c], 'seq', ahead + back))]
    ppermute x17, waiting for transfers between devices: 15.7 us -> 17.3 us  [swapped(): lax.ppermute(value, axis, [(i, i ^ bit) for i in range(lax.axis_size(axis...]
    ppermute x17, starting transfers between devices: 18.2 us -> 19.5 us  [swapped(): lax.ppermute(value, axis, [(i, i ^ bit) for i in range(lax.axis_size(axis...]
  transfers between devices with their start and end apart: 21 -> 21, of which waited for: 7 -> 7; matrix products, arithmetic and copies ran while one was open for 5% -> 3% of each run, Pallas kernels for 13% -> 13%
where the time goes in v2:
time: 73.5 us; the launch traced here: 73.2 us
  starting transfers between devices  31.2 us (42%)
  Pallas kernels  19.5 us (27%)
  waiting for transfers between devices  17.3 us (24%)
  other arithmetic  3.5 us (5%)
  between operations  0.99 us (1%)
    ppermute x17, starting transfers between devices, swapped(): lax.ppermute(value, axis, [(i, i ^ bit) for i in range(lax.axis_size(axis...  19.5 us
    ppermute x17, waiting for transfers between devices, swapped(): lax.ppermute(value, axis, [(i, i ^ bit) for i in range(lax.axis_size(axis...  17.3 us
    pallas_call x2, Pallas kernels, work(): pl.pallas_call(functools.partial(main_kernel, size, groups, filter_len, f...  17 us
    ppermute x2, starting transfers between devices, work(): s3.append(lax.ppermute(e1[c], 'seq', ahead + back))  10.3 us
    select_n x2, other arithmetic, gives(): jnp.where(par == 0, columns(g_all, 1, chunk), columns(x_all, 0, chunk))  2.21 us
    pallas_call x1, Pallas kernels, work(): pl.pallas_call(prep_kernel, in_specs=[vmem] * 7, out_specs=[vmem] * 7, ou...  1.75 us
  transfers between devices with their start and end apart: 21, of which 7 were waited for; matrix products, arithmetic and copies ran while one was open for 3% of the time, Pallas kernels for 13%

profile of v2, /device:TPU:0, one launch (start us, length us, event | category | flops | bytes accessed | tf_op | source)
XLA Modules:
  0.0 73.2 jit_solution(7284594069033905145)
XLA Ops:
  0.6 0.0 copy-start
  0.7 1.1 %slice_select_fusion.7 = bf16[512,256]{1,0:T(8,128)(2,1)S(1)} fusion(bf16[512,1024]{1,0:T(8,128)(2,1)} %xk_ref.1, bf16[512,1024]{1,0:T(8,128)(2,1)} %gk_ref.1, pred[]{:T(512)S(6)} %eq.7), kind=kLoop, calls=%fused_computation.7 | loop fusion | flops 131072 | bytes 786433 | tf_op jit(solution)/shard_map/jit(_where)/select_n | solution.py:373
  1.8 0.0 copy-start.1
  1.8 3.1 %collective-permute-start = (bf16[512,256]{1,0:T(8,128)(2,1)S(1)}, bf16[512,256]{1,0:T(8,128)(2,1)S(1)}, u32[]{:S(2)}, u32[]{:S(2)}) collective-permute-start(bf16[512,256]{1,0:T(8,128)(2,1)S(1)} %slice_select_fusion.7), channel_id=1, source_target_pairs={{0,4},{4,0},{8,12},{12,8},{16,20},{20,16},{24,28},{28,24},{1,5},{5... | collective-permute-start | bytes 786440 | tf_op jit(solution)/shard_map/ppermute | solution.py:18
  4.9 1.1 %slice_select_fusion.6 = bf16[512,256]{1,0:T(8,128)(2,1)S(1)} fusion(bf16[512,1024]{1,0:T(8,128)(2,1)} %xk_ref.1, bf16[512,1024]{1,0:T(8,128)(2,1)} %gk_ref.1, pred[]{:T(512)S(6)} %eq.7), kind=kLoop, calls=%fused_computation.6 | loop fusion | flops 131072 | bytes 786433 | tf_op jit(solution)/shard_map/jit(_where)/select_n | solution.py:373
  6.0 0.2 collective-permute-start.1
  6.1 1.1 %broadcast_select_fusion.2 = (bf16[512,256]{1,0:T(8,128)(2,1)S(1)}, bf16[512,256]{1,0:T(8,128)(2,1)S(1)}) fusion(pred[]{:T(512)S(6)} %eq.8, bf16[512,1024]{1,0:T(8,128)(2,1)S(1)} %copy-done, pred[]{:T(512)S(6)} %eq.7, bf16[512,1024]{1,0:T(8,128)(2,1)} %gk_ref.1), kind=kLoop, calls=%fused_computation.10 | loop fusion | flops 524288 | bytes 1572866 | tf_op jit(solution)/shard_map/jit(_where)/select_n | solution.py:386
  7.2 2.1 %collective-permute-start.7 = (bf16[512,256]{1,0:T(8,128)(2,1)S(1)}, bf16[512,256]{1,0:T(8,128)(2,1)S(1)}, u32[]{:S(2)}, u32[]{:S(2)}) collective-permute-start(bf16[512,256]{1,0:T(8,128)(2,1)S(1)} %get-tuple-element.77), channel_id=1, source_target_pairs={{0,8},{4,12},{8,0},{12,4},{16,24},{20,28},{24,16},{28,20},{1,9},{5... | collective-permute-start | bytes 786440 | tf_op jit(solution)/shard_map/ppermute | solution.py:18
  9.3 0.7 collective-permute-start.8
  9.9 0.0 copy-done.1
  9.9 0.0 copy-start.12
  10.0 0.1 broadcast_select_fusion
  10.0 0.0 copy-start.11
  10.1 0.0 copy-start.2
  10.1 0.0 copy-start.3
  10.1 0.0 copy-start.4
  10.1 0.0 copy-start.8
  10.1 0.0 copy-start.9
  10.1 0.1 slice_select_fusion
  10.2 1.9 %collective-permute-done.e1_ref = bf16[512,256]{1,0:T(8,128)(2,1)S(1)} collective-permute-done((bf16[512,256]{1,0:T(8,128)(2,1)S(1)}, bf16[512,256]{1,0:T(8,128)(2,1)S(1)}, u32[]{:S(2)}, u32[]{:S(2)}) %collective-permute-start) | collective-permute-done | bytes 262176 | tf_op jit(solution)/shard_map/ppermute | solution.py:18
  12.0 2.0 %collective-permute-start.6 = (bf16[512,256]{1,0:T(8,128)(2,1)S(1)}, bf16[512,256]{1,0:T(8,128)(2,1)S(1)}, u32[]{:S(2)}, u32[]{:S(2)}) collective-permute-start(bf16[512,256]{1,0:T(8,128)(2,1)S(1)} %get-tuple-element.53), channel_id=1, source_target_pairs={{0,4},{4,0},{8,12},{12,8},{16,20},{20,16},{24,28},{28,24},{1,5},{5... | collective-permute-start | bytes 786440 | tf_op jit(solution)/shard_map/ppermute | solution.py:18
  14.1 4.0 %collective-permute-start.9 = (bf16[512,256]{1,0:T(8,128)(2,1)S(1)}, bf16[512,256]{1,0:T(8,128)(2,1)S(1)}, u32[]{:S(2)}, u32[]{:S(2)}) collective-permute-start(bf16[512,256]{1,0:T(8,128)(2,1)S(1)} %collective-permute-done.e1_ref), channel_id=1, source_target_pairs={{0,8},{8,16},{16,24},{12,4},{20,12},{28,20},{1,9},{9,17},{17,25},{... | collective-permute-start | bytes 786440 | tf_op jit(solution)/shard_map/ppermute | solution.py:401
  18.1 0.0 collective-permute-done.1.e1_ref
  18.1 1.7 %collective-permute-start.3 = (bf16[512,256]{1,0:T(8,128)(2,1)S(1)}, bf16[512,256]{1,0:T(8,128)(2,1)S(1)}, u32[]{:S(2)}, u32[]{:S(2)}) collective-permute-start(bf16[512,256]{1,0:T(8,128)(2,1)S(1)} %get-tuple-element.75), channel_id=1, source_target_pairs={{0,8},{4,12},{8,0},{12,4},{16,24},{20,28},{24,16},{28,20},{1,9},{5... | collective-permute-start | bytes 786440 | tf_op jit(solution)/shard_map/ppermute | solution.py:18
  19.8 0.6 copy-done.5
  20.4 0.0 copy-done.6
  20.4 0.0 copy-done.7
  20.4 1.7 %prep.1 = (bf16[256,1536]{1,0:T(8,128)(2,1)S(1)}, f32[64,1536]{1,0:T(8,128)S(1)}, f32[64,1536]{1,0:T(8,128)S(1)}, f32[64,1536]{1,0:T(8,128)S(1)}, f32[64,1536]{1...) custom-call(f32[17,64]{1,0:T(8,128)S(1)} %copy-done.4, f32[1,64]{1,0:T(1,128)S(1)} %bitcast.10, ...), custom_call_target="tpu_custom_call" | custom-call | tf_op jit(solution)/shard_map/prep/pallas_call | solution.py:409
  22.2 0.0 collective-permute-done.7.za_ref
  22.2 0.7 collective-permute-start.4
  22.9 0.0 collective-permute-done.8.zb_ref
  22.9 1.6 %collective-permute-start.2 = (bf16[512,256]{1,0:T(8,128)(2,1)S(1)}, bf16[512,256]{1,0:T(8,128)(2,1)S(1)}, u32[]{:S(2)}, u32[]{:S(2)}) collective-permute-start(bf16[512,256]{1,0:T(8,128)(2,1)S(1)} %get-tuple-element.50), channel_id=1, source_target_pairs={{0,4},{4,0},{8,12},{12,8},{16,20},{20,16},{24,28},{28,24},{1,5},{5... | collective-permute-start | bytes 786440 | tf_op jit(solution)/shard_map/ppermute | solution.py:18
  24.5 0.0 collective-permute-done.6.e2_ref
  24.5 6.3 %collective-permute-start.5 = (bf16[512,256]{1,0:T(8,128)(2,1)S(1)}, bf16[512,256]{1,0:T(8,128)(2,1)S(1)}, u32[]{:S(2)}, u32[]{:S(2)}) collective-permute-start(bf16[512,256]{1,0:T(8,128)(2,1)S(1)} %collective-permute-done.1.e1_ref), channel_id=1, source_target_pairs={{0,8},{8,16},{16,24},{12,4},{20,12},{28,20},{1,9},{9,17},{17,25},{... | collective-permute-start | bytes 786440 | tf_op jit(solution)/shard_map/ppermute | solution.py:401
  30.8 0.0 collective-permute-done.9.s3_ref
  30.8 8.1 %filter_grad.2 = (f32[72,256]{1,0:T(8,128)S(1)}, f32[64,1536]{1,0:T(8,128)S(1)}) custom-call(bf16[512,1024]{1,0:T(8,128)(2,1)S(1)} %copy-done, bf16[512,1024]{1,0:T(8,128)(2,1)S(1)} %copy-done.1, bf16[512,256]{1,0:T(8,128)(2,1)S(1)} %collective-permute-done.e1_ref, bf16[512,256]{1,0:T(8,128)(2,1)S(1)} %collective-permute-done.6.e2_ref, ...), custom_call_target="tpu_custom_call" | custom-call | flops 4000000000 | bytes 8388608 | tf_op jit(solution)/shard_map/filter_grad/pallas_call | solution.py:487
  38.9 0.0 collective-permute-done.3.za_ref
  38.9 0.0 collective-permute-done.4.zb_ref
  38.9 0.0 collective-permute-done.2.e2_ref
  39.0 0.0 collective-permute-done.5.s3_ref
  39.0 8.9 %filter_grad.3 = (f32[72,256]{1,0:T(8,128)S(1)}, f32[64,128]{1,0:T(8,128)S(1)}) custom-call(bf16[512,1024]{1,0:T(8,128)(2,1)S(1)} %copy-done, bf16[512,1024]{1,0:T(8,128)(2,1)S(1)} %copy-done.1, bf16[512,256]{1,0:T(8,128)(2,1)S(1)} %collective-permute-done.1.e1_ref, bf16[512,256]{1,0:T(8,128)(2,1)S(1)} %collective-permute-done.2.e2_ref, ...), custom_call_target="tpu_custom_call" | custom-call | flops 4000000000 | bytes 8388608 | tf_op jit(solution)/shard_map/filter_grad/pallas_call | solution.py:487
  47.9 0.1 collective-permute-start.18
  47.9 2.0 %collective-permute-start.15 = (f32[72,256]{1,0:T(8,128)S(1)}, f32[72,256]{1,0:T(8,128)S(1)}, u32[]{:S(2)}, u32[]{:S(2)}) collective-permute-start(f32[72,256]{1,0:T(8,128)S(1)} %get-tuple-element.62), channel_id=1, source_target_pairs={{0,8},{4,12},{8,0},{12,4},{16,24},{20,28},{24,16},{28,20},{1,9},{5... | collective-permute-start | bytes 221192 | tf_op jit(solution)/shard_map/ppermute | solution.py:18
  49.9 0.0 collective-permute-start.10
  49.9 2.3 %collective-permute-done.18 = f32[72,256]{1,0:T(8,128)S(1)} collective-permute-done((f32[72,256]{1,0:T(8,128)S(1)}, f32[72,256]{1,0:T(8,128)S(1)}, u32[]{:S(2)}, u32[]{:S(2)}) %collective-permute-start.18) | collective-permute-done | bytes 73760 | tf_op jit(solution)/shard_map/ppermute | solution.py:18
  52.3 0.1 collective-permute-start.19
  52.4 0.7 collective-permute-done.15
  53.1 2.3 %collective-permute-start.16 = (f32[72,256]{1,0:T(8,128)S(1)}, f32[72,256]{1,0:T(8,128)S(1)}, u32[]{:S(2)}, u32[]{:S(2)}) collective-permute-start(f32[72,256]{1,0:T(8,128)S(1)} %add.38), channel_id=1, source_target_pairs={{0,16},{4,20},{8,24},{12,28},{16,0},{20,4},{24,8},{28,12},{1,17},{... | collective-permute-start | bytes 221192 | tf_op jit(solution)/shard_map/ppermute | solution.py:18
  55.4 0.0 collective-permute-done.10
  55.4 1.6 %collective-permute-start.11 = (f32[64,128]{1,0:T(8,128)S(1)}, f32[64,128]{1,0:T(8,128)S(1)}, u32[]{:S(2)}, u32[]{:S(2)}) collective-permute-start(f32[64,128]{1,0:T(8,128)S(1)} %add.34), channel_id=1, source_target_pairs={{0,2},{1,3},{2,0},{3,1},{4,6},{5,7},{6,4},{7,5},{8,10},{9,11},{10,... | collective-permute-start | bytes 98312 | tf_op jit(solution)/shard_map/ppermute | solution.py:18
  56.9 2.4 %collective-permute-done.11 = f32[64,128]{1,0:T(8,128)S(1)} collective-permute-done((f32[64,128]{1,0:T(8,128)S(1)}, f32[64,128]{1,0:T(8,128)S(1)}, u32[]{:S(2)}, u32[]{:S(2)}) %collective-permute-start.11) | collective-permute-done | bytes 32800 | tf_op jit(solution)/shard_map/ppermute | solution.py:18
  59.4 0.0 collective-permute-start.12
  59.4 0.0 collective-permute-done.19
  59.4 1.8 %collective-permute-start.20 = (f32[72,256]{1,0:T(8,128)S(1)}, f32[72,256]{1,0:T(8,128)S(1)}, u32[]{:S(2)}, u32[]{:S(2)}) collective-permute-start(f32[72,256]{1,0:T(8,128)S(1)} %add.41.rest_2_), channel_id=1, source_target_pairs={{0,4},{4,0},{8,12},{12,8},{16,20},{20,16},{24,28},{28,24},{1,5},{5... | collective-permute-start | bytes 221192 | tf_op jit(solution)/shard_map/ppermute | solution.py:18
  61.2 0.0 collective-permute-done.16
  61.2 0.4 collective-permute-start.17
  61.6 2.1 %collective-permute-done.12 = f32[64,128]{1,0:T(8,128)S(1)} collective-permute-done((f32[64,128]{1,0:T(8,128)S(1)}, f32[64,128]{1,0:T(8,128)S(1)}, u32[]{:S(2)}, u32[]{:S(2)}) %collective-permute-start.12) | collective-permute-done | bytes 32800 | tf_op jit(solution)/shard_map/ppermute | solution.py:18
  63.6 0.6 collective-permute-start.13
  64.3 4.2 %collective-permute-done.13 = f32[64,128]{1,0:T(8,128)S(1)} collective-permute-done((f32[64,128]{1,0:T(8,128)S(1)}, f32[64,128]{1,0:T(8,128)S(1)}, u32[]{:S(2)}, u32[]{:S(2)}) %collective-permute-start.13) | collective-permute-done | bytes 32800 | tf_op jit(solution)/shard_map/ppermute | solution.py:18
  68.4 0.2 collective-permute-start.14
  68.6 3.7 %collective-permute-done.14.far_ref = f32[64,128]{1,0:T(8,128)S(1)} collective-permute-done((f32[64,128]{1,0:T(8,128)S(1)}, f32[64,128]{1,0:T(8,128)S(1)}, u32[]{:S(2)}, u32[]{:S(2)}) %collective-permute-start.14) | collective-permute-done | bytes 32800 | tf_op jit(solution)/shard_map/ppermute | solution.py:18
  72.4 0.0 collective-permute-done.20.rest_3_
  72.4 0.0 collective-permute-done.17.rest_1_
  72.4 0.8 %finish.1 = (f32[17,64]{1,0:T(8,128)}, f32[1,64]{1,0:T(1,128)}, f32[1,64]{1,0:T(1,128)}, f32[64,64]{1,0:T(8,128)}, f32[1,64]{1,0:T(1,128)}, /*index=5*/f32[1,64]...) custom-call(f32[64,128]{1,0:T(8,128)S(1)} %add.37.net_ref, f32[64,128]{1,0:T(8,128)S(1)} %collective-permute-done.14.far_ref, ...), custom_call_target="tpu_custom_call" | custom-call | tf_op jit(solution)/shard_map/finish/pallas_call | solution.py:518
  (21 shorter events, 0.1 us)
Async XLA Ops:
  0.6 5.5 %copy-start = (bf16[512,1024]{1,0:T(8,128)(2,1)S(1)}, bf16[512,1024]{1,0:T(8,128)(2,1)}, u32[]{:S(2)}) copy-start(bf16[512,1024]{1,0:T(8,128)(2,1)} %xk_ref.1) | copy-start | bytes 3145732
  1.8 8.1 %copy-start.1 = (bf16[512,1024]{1,0:T(8,128)(2,1)S(1)}, bf16[512,1024]{1,0:T(8,128)(2,1)}, u32[]{:S(2)}) copy-start(bf16[512,1024]{1,0:T(8,128)(2,1)} %gk_ref.1) | copy-start | bytes 3145732
  1.8 10.2 %collective-permute-start = (bf16[512,256]{1,0:T(8,128)(2,1)S(1)}, bf16[512,256]{1,0:T(8,128)(2,1)S(1)}, u32[]{:S(2)}, u32[]{:S(2)}) collective-permute-start(bf16[512,256]{1,0:T(8,128)(2,1)S(1)} %slice_select_fusion.7), channel_id=1, source_target_pairs={{0,4},{4,0},{8,12},{12,8},{16,20},{20,16},{24,28},{28,24},{1,5},{5... | collective-permute-start | bytes 786440 | tf_op jit(solution)/shard_map/ppermute | solution.py:18
  6.0 12.1 %collective-permute-start.1 = (bf16[512,256]{1,0:T(8,128)(2,1)S(1)}, bf16[512,256]{1,0:T(8,128)(2,1)S(1)}, u32[]{:S(2)}, u32[]{:S(2)}) collective-permute-start(bf16[512,256]{1,0:T(8,128)(2,1)S(1)} %slice_select_fusion.6), channel_id=1, source_target_pairs={{0,4},{4,0},{8,12},{12,8},{16,20},{20,16},{24,28},{28,24},{1,5},{5... | collective-permute-start | bytes 786440 | tf_op jit(solution)/shard_map/ppermute | solution.py:18
  7.2 15.0 %collective-permute-start.7 = (bf16[512,256]{1,0:T(8,128)(2,1)S(1)}, bf16[512,256]{1,0:T(8,128)(2,1)S(1)}, u32[]{:S(2)}, u32[]{:S(2)}) collective-permute-start(bf16[512,256]{1,0:T(8,128)(2,1)S(1)} %get-tuple-element.77), channel_id=1, source_target_pairs={{0,8},{4,12},{8,0},{12,4},{16,24},{20,28},{24,16},{28,20},{1,9},{5... | collective-permute-start | bytes 786440 | tf_op jit(solution)/shard_map/ppermute | solution.py:18
  9.3 13.6 %collective-permute-start.8 = (bf16[512,256]{1,0:T(8,128)(2,1)S(1)}, bf16[512,256]{1,0:T(8,128)(2,1)S(1)}, u32[]{:S(2)}, u32[]{:S(2)}) collective-permute-start(bf16[512,256]{1,0:T(8,128)(2,1)S(1)} %get-tuple-element.76), channel_id=1, source_target_pairs={{8,16},{12,20},{16,8},{20,12},{9,17},{13,21},{17,9},{21,13},{10,18... | collective-permute-start | bytes 786440 | tf_op jit(solution)/shard_map/ppermute | solution.py:397
  9.9 20.8 %copy-start.12 = (bf16[2,256,256]{2,1,0:T(8,128)(2,1)S(1)}, bf16[2,256,256]{2,1,0:T(8,128)(2,1)}, u32[]{:S(2)}) copy-start(bf16[2,256,256]{2,1,0:T(8,128)(2,1)} %constant.43.clone.inv_ref) | copy-start | bytes 786436
  10.0 20.8 %copy-start.11 = (bf16[2,1024,256]{2,1,0:T(8,128)(2,1)S(1)}, bf16[2,1024,256]{2,1,0:T(8,128)(2,1)}, u32[]{:S(2)}) copy-start(bf16[2,1024,256]{2,1,0:T(8,128)(2,1)} %constant.42.clone.fwd_ref) | copy-start | bytes 3145732
  10.1 9.7 %copy-start.2 = (f32[17,1536]{1,0:T(8,128)S(1)}, f32[17,1536]{1,0:T(8,128)}, u32[]{:S(2)}) copy-start(f32[17,1536]{1,0:T(8,128)} %constant.41.clone.feats_ref.rest_3_) | copy-start | bytes 313348
  10.1 9.7 %copy-start.3 = (f32[64,64]{1,0:T(8,128)S(1)}, f32[64,64]{1,0:T(8,128)}, u32[]{:S(2)}) copy-start(f32[64,64]{1,0:T(8,128)} %rest_1_.1) | copy-start | bytes 49156
  10.1 9.7 %copy-start.4 = (f32[17,64]{1,0:T(8,128)S(1)}, f32[17,64]{1,0:T(8,128)}, u32[]{:S(2)}) copy-start(f32[17,64]{1,0:T(8,128)} %ew_ref) | copy-start | bytes 13060
  10.1 9.7 %copy-start.8 = (f32[64]{0:T(128)S(1)}, f32[64]{0:T(128)}, u32[]{:S(2)}) copy-start(f32[64]{0:T(128)} %param.20) | copy-start | bytes 772
  10.1 20.7 %copy-start.9 = (f32[64,1024]{1,0:T(8,128)S(1)}, f32[64,1024]{1,0:T(8,128)}, u32[]{:S(2)}) copy-start(f32[64,1024]{1,0:T(8,128)} %head_ref.3) | copy-start | bytes 786436
  12.0 12.4 %collective-permute-start.6 = (bf16[512,256]{1,0:T(8,128)(2,1)S(1)}, bf16[512,256]{1,0:T(8,128)(2,1)S(1)}, u32[]{:S(2)}, u32[]{:S(2)}) collective-permute-start(bf16[512,256]{1,0:T(8,128)(2,1)S(1)} %get-tuple-element.53), channel_id=1, source_target_pairs={{0,4},{4,0},{8,12},{12,8},{16,20},{20,16},{24,28},{28,24},{1,5},{5... | collective-permute-start | bytes 786440 | tf_op jit(solution)/shard_map/ppermute | solution.py:18
  14.1 16.7 %collective-permute-start.9 = (bf16[512,256]{1,0:T(8,128)(2,1)S(1)}, bf16[512,256]{1,0:T(8,128)(2,1)S(1)}, u32[]{:S(2)}, u32[]{:S(2)}) collective-permute-start(bf16[512,256]{1,0:T(8,128)(2,1)S(1)} %collective-permute-done.e1_ref), channel_id=1, source_target_pairs={{0,8},{8,16},{16,24},{12,4},{20,12},{28,20},{1,9},{9,17},{17,25},{... | collective-permute-start | bytes 786440 | tf_op jit(solution)/shard_map/ppermute | solution.py:401
  18.1 20.8 %collective-permute-start.3 = (bf16[512,256]{1,0:T(8,128)(2,1)S(1)}, bf16[512,256]{1,0:T(8,128)(2,1)S(1)}, u32[]{:S(2)}, u32[]{:S(2)}) collective-permute-start(bf16[512,256]{1,0:T(8,128)(2,1)S(1)} %get-tuple-element.75), channel_id=1, source_target_pairs={{0,8},{4,12},{8,0},{12,4},{16,24},{20,28},{24,16},{28,20},{1,9},{5... | collective-permute-start | bytes 786440 | tf_op jit(solution)/shard_map/ppermute | solution.py:18
  19.7 0.7 copy-start.5
  19.7 0.7 copy-start.6
  19.7 0.7 copy-start.7
  20.4 10.4 %copy-start.10 = (f32[1024]{0:T(1024)S(1)}, f32[1024]{0:T(1024)}, u32[]{:S(2)}) copy-start(f32[1024]{0:T(1024)} %param.22) | copy-start | bytes 12292
  22.2 16.7 %collective-permute-start.4 = (bf16[512,256]{1,0:T(8,128)(2,1)S(1)}, bf16[512,256]{1,0:T(8,128)(2,1)S(1)}, u32[]{:S(2)}, u32[]{:S(2)}) collective-permute-start(bf16[512,256]{1,0:T(8,128)(2,1)S(1)} %get-tuple-element.74), channel_id=1, source_target_pairs={{8,16},{12,20},{16,8},{20,12},{9,17},{13,21},{17,9},{21,13},{10,18... | collective-permute-start | bytes 786440 | tf_op jit(solution)/shard_map/ppermute | solution.py:397
  22.9 16.1 %collective-permute-start.2 = (bf16[512,256]{1,0:T(8,128)(2,1)S(1)}, bf16[512,256]{1,0:T(8,128)(2,1)S(1)}, u32[]{:S(2)}, u32[]{:S(2)}) collective-permute-start(bf16[512,256]{1,0:T(8,128)(2,1)S(1)} %get-tuple-element.50), channel_id=1, source_target_pairs={{0,4},{4,0},{8,12},{12,8},{16,20},{20,16},{24,28},{28,24},{1,5},{5... | collective-permute-start | bytes 786440 | tf_op jit(solution)/shard_map/ppermute | solution.py:18
  24.5 14.5 %collective-permute-start.5 = (bf16[512,256]{1,0:T(8,128)(2,1)S(1)}, bf16[512,256]{1,0:T(8,128)(2,1)S(1)}, u32[]{:S(2)}, u32[]{:S(2)}) collective-permute-start(bf16[512,256]{1,0:T(8,128)(2,1)S(1)} %collective-permute-done.1.e1_ref), channel_id=1, source_target_pairs={{0,8},{8,16},{16,24},{12,4},{20,12},{28,20},{1,9},{9,17},{17,25},{... | collective-permute-start | bytes 786440 | tf_op jit(solution)/shard_map/ppermute | solution.py:401
  47.9 4.4 %collective-permute-start.18 = (f32[72,256]{1,0:T(8,128)S(1)}, f32[72,256]{1,0:T(8,128)S(1)}, u32[]{:S(2)}, u32[]{:S(2)}) collective-permute-start(f32[72,256]{1,0:T(8,128)S(1)} %get-tuple-element.63), channel_id=1, source_target_pairs={{0,8},{4,12},{8,0},{12,4},{16,24},{20,28},{24,16},{28,20},{1,9},{5... | collective-permute-start | bytes 221192 | tf_op jit(solution)/shard_map/ppermute | solution.py:18
  47.9 5.1 %collective-permute-start.15 = (f32[72,256]{1,0:T(8,128)S(1)}, f32[72,256]{1,0:T(8,128)S(1)}, u32[]{:S(2)}, u32[]{:S(2)}) collective-permute-start(f32[72,256]{1,0:T(8,128)S(1)} %get-tuple-element.62), channel_id=1, source_target_pairs={{0,8},{4,12},{8,0},{12,4},{16,24},{20,28},{24,16},{28,20},{1,9},{5... | collective-permute-start | bytes 221192 | tf_op jit(solution)/shard_map/ppermute | solution.py:18
  49.9 5.4 %collective-permute-start.10 = (f32[64,128]{1,0:T(8,128)S(1)}, f32[64,128]{1,0:T(8,128)S(1)}, u32[]{:S(2)}, u32[]{:S(2)}) collective-permute-start(f32[64,128]{1,0:T(8,128)S(1)} %get-tuple-element.61), channel_id=1, source_target_pairs={{0,1},{1,0},{2,3},{3,2},{4,5},{5,4},{6,7},{7,6},{8,9},{9,8},{10,11... | collective-permute-start | bytes 98312 | tf_op jit(solution)/shard_map/ppermute | solution.py:18
  52.3 7.1 %collective-permute-start.19 = (f32[72,256]{1,0:T(8,128)S(1)}, f32[72,256]{1,0:T(8,128)S(1)}, u32[]{:S(2)}, u32[]{:S(2)}) collective-permute-start(f32[72,256]{1,0:T(8,128)S(1)} %add.40), channel_id=1, source_target_pairs={{0,16},{4,20},{8,24},{12,28},{16,0},{20,4},{24,8},{28,12},{1,17},{... | collective-permute-start | bytes 221192 | tf_op jit(solution)/shard_map/ppermute | solution.py:18
  53.1 8.1 %collective-permute-start.16 = (f32[72,256]{1,0:T(8,128)S(1)}, f32[72,256]{1,0:T(8,128)S(1)}, u32[]{:S(2)}, u32[]{:S(2)}) collective-permute-start(f32[72,256]{1,0:T(8,128)S(1)} %add.38), channel_id=1, source_target_pairs={{0,16},{4,20},{8,24},{12,28},{16,0},{20,4},{24,8},{28,12},{1,17},{... | collective-permute-start | bytes 221192 | tf_op jit(solution)/shard_map/ppermute | solution.py:18
  55.4 4.0 %collective-permute-start.11 = (f32[64,128]{1,0:T(8,128)S(1)}, f32[64,128]{1,0:T(8,128)S(1)}, u32[]{:S(2)}, u32[]{:S(2)}) collective-permute-start(f32[64,128]{1,0:T(8,128)S(1)} %add.34), channel_id=1, source_target_pairs={{0,2},{1,3},{2,0},{3,1},{4,6},{5,7},{6,4},{7,5},{8,10},{9,11},{10,... | collective-permute-start | bytes 98312 | tf_op jit(solution)/shard_map/ppermute | solution.py:18
  59.4 4.3 %collective-permute-start.12 = (f32[64,128]{1,0:T(8,128)S(1)}, f32[64,128]{1,0:T(8,128)S(1)}, u32[]{:S(2)}, u32[]{:S(2)}) collective-permute-start(f32[64,128]{1,0:T(8,128)S(1)} %add.35), channel_id=1, source_target_pairs={{0,8},{4,12},{8,0},{12,4},{16,24},{20,28},{24,16},{28,20},{1,9},{5... | collective-permute-start | bytes 98312 | tf_op jit(solution)/shard_map/ppermute | solution.py:18
  59.4 13.0 %collective-permute-start.20 = (f32[72,256]{1,0:T(8,128)S(1)}, f32[72,256]{1,0:T(8,128)S(1)}, u32[]{:S(2)}, u32[]{:S(2)}) collective-permute-start(f32[72,256]{1,0:T(8,128)S(1)} %add.41.rest_2_), channel_id=1, source_target_pairs={{0,4},{4,0},{8,12},{12,8},{16,20},{20,16},{24,28},{28,24},{1,5},{5... | collective-permute-start | bytes 221192 | tf_op jit(solution)/shard_map/ppermute | solution.py:18
  61.2 11.2 %collective-permute-start.17 = (f32[72,256]{1,0:T(8,128)S(1)}, f32[72,256]{1,0:T(8,128)S(1)}, u32[]{:S(2)}, u32[]{:S(2)}) collective-permute-start(f32[72,256]{1,0:T(8,128)S(1)} %add.39.rest_0_), channel_id=1, source_target_pairs={{0,4},{4,0},{8,12},{12,8},{16,20},{20,16},{24,28},{28,24},{1,5},{5... | collective-permute-start | bytes 221192 | tf_op jit(solution)/shard_map/ppermute | solution.py:18
  63.6 4.8 %collective-permute-start.13 = (f32[64,128]{1,0:T(8,128)S(1)}, f32[64,128]{1,0:T(8,128)S(1)}, u32[]{:S(2)}, u32[]{:S(2)}) collective-permute-start(f32[64,128]{1,0:T(8,128)S(1)} %add.36), channel_id=1, source_target_pairs={{0,16},{4,20},{8,24},{12,28},{16,0},{20,4},{24,8},{28,12},{1,17},{... | collective-permute-start | bytes 98312 | tf_op jit(solution)/shard_map/ppermute | solution.py:18
  68.4 3.9 %collective-permute-start.14 = (f32[64,128]{1,0:T(8,128)S(1)}, f32[64,128]{1,0:T(8,128)S(1)}, u32[]{:S(2)}, u32[]{:S(2)}) collective-permute-start(f32[64,128]{1,0:T(8,128)S(1)} %add.37.net_ref), channel_id=1, source_target_pairs={{0,4},{4,0},{8,12},{12,8},{16,20},{20,16},{24,28},{28,24},{1,5},{5... | collective-permute-start | bytes 98312 | tf_op jit(solution)/shard_map/ppermute | solution.py:18

commit v3 on v2

--- a/solution.py
+++ b/solution.py
@@ -199,14 +199,16 @@
     ]
     copies = [
         pltpu.make_async_copy(source, stage.at[i], sems.at[i])
-        for i, (source, _) in enumerate(sources)
+        for i, (source, _) in enumerate(sources[:2])
     ]
     for copy in copies:
         copy.start()
-    for n, (_, slot) in enumerate(sources):
-        copies[n].wait()
+    for n, (ref, slot) in enumerate(sources[2:] + sources[:2]):
+        if n >= 5:
+            copies[n - 5].wait()
+            ref = stage.at[n - 5]
         for i in range(2):
-            block = stage[n, i * size : (i + 1) * size, :]
+            block = ref[i * size : (i + 1) * size, :]
             both = dot16(fwd_ref[par], block)
             spec[slot + (i ^ par)] = both[: 2 * size] + both[2 * size :]
 
@@ -269,7 +271,10 @@
                 prod[2 * m + 1, at[0], at[1]] = low
         return carry
 
-    lax.fori_loop(0, tiles * (width // lanes), body, 0)
+    def two(it, carry):
+        return body(2 * it + 1, body(2 * it, carry))
+
+    lax.fori_loop(0, tiles * (width // lanes) // 2, two, 0)
 
     rates = rates_ref[:, here]
     tap = lax.broadcasted_iota(jnp.int32, (size, width), 0)
@@ -462,8 +467,8 @@
         part_shape = jax.ShapeDtypeStruct((hidden + 8, width), jnp.float32)
         second_shape = jax.ShapeDtypeStruct((hidden, filter_len), jnp.float32)
         scratch = [
-            pltpu.VMEM((7, block_len, width), jnp.bfloat16),
-            pltpu.SemaphoreType.DMA((7,)),
+            pltpu.VMEM((2, block_len, width), jnp.bfloat16),
+            pltpu.SemaphoreType.DMA((2,)),
             pltpu.VMEM((14, 2 * size, width), jnp.float32),
             pltpu.VMEM((2 * groups, 2 * size, width), jnp.bfloat16),
             pltpu.VMEM((2 * groups, 16, 128), jnp.float32),
@@ -486,8 +491,8 @@
             out_shape = [part_shape, second_shape]
         part, out = pl.pallas_call(
             functools.partial(main_kernel, size, groups, filter_len, first, last, c),
-            in_specs=[pl.BlockSpec(memory_space=pltpu.HBM)] * 7
-            + [pl.BlockSpec(memory_space=pltpu.VMEM)] * (len(operands) - 7),
+            in_specs=[pl.BlockSpec(memory_space=pltpu.HBM)] * 2
+            + [pl.BlockSpec(memory_space=pltpu.VMEM)] * (len(operands) - 2),
             out_specs=[pl.BlockSpec(memory_space=pltpu.VMEM)] * 2,
             out_shape=out_shape,
             scratch_shapes=scratch,
@@ -504,10 +509,10 @@
             second_grad = out
 
     far_bits = bits_of("seq", 2)
-    steps = [("chan", b) for b in bits_of("chan")] + [("seq", b) for b in far_bits]
-    for axis, bit in steps:
-        net = net + swapped(net, axis, bit)
-    far = swapped(net, "seq", 1)
+    steps = [("chan", b) for b in bits_of("chan")] + [("seq", b) for b in bits_of("seq")]
+    for i, (axis, bit) in enumerate(steps):
+        far = swapped(net, axis, bit)
+        net = net + far if i < len(steps) - 1 else net
     both = []
     for p in parts:
         for bit in far_bits:

time: 73.5 us -> 71.2 us (0.969)
  Pallas kernels: 19.5 us -> 17.6 us
  waiting for transfers between devices: 17.3 us -> 16.4 us
    pallas_call x2, Pallas kernels: 17 us -> 15.1 us  [work(): pl.pallas_call(functools.partial(main_kernel, size, groups, filter_len, f...]
    ppermute x17, waiting for transfers between devices: 17.3 us -> 16.4 us  [swapped(): lax.ppermute(value, axis, [(i, i ^ bit) for i in range(lax.axis_size(axis...]
  transfers between devices with their start and end apart: 21 -> 21, of which waited for: 7 -> 7; matrix products, arithmetic and copies ran while one was open for 3% -> 3% of each run, Pallas kernels for 13% -> 12%
where the time goes in v3:
time: 71.2 us; the launch traced here: 71 us
  starting transfers between devices  31.8 us (45%)
  Pallas kernels  17.6 us (25%)
  waiting for transfers between devices  16.4 us (23%)
  other arithmetic  3.5 us (5%)
  between operations  0.97 us (1%)
    ppermute x17, starting transfers between devices, swapped(): lax.ppermute(value, axis, [(i, i ^ bit) for i in range(lax.axis_size(axis...  20.1 us
    ppermute x17, waiting for transfers between devices, swapped(): lax.ppermute(value, axis, [(i, i ^ bit) for i in range(lax.axis_size(axis...  16.4 us
    pallas_call x2, Pallas kernels, work(): pl.pallas_call(functools.partial(main_kernel, size, groups, filter_len, f...  15.1 us
    ppermute x2, starting transfers between devices, work(): s3.append(lax.ppermute(e1[c], 'seq', ahead + back))  10.3 us
    select_n x2, other arithmetic, gives(): jnp.where(par == 0, columns(g_all, 1, chunk), columns(x_all, 0, chunk))  2.21 us
    pallas_call x1, Pallas kernels, work(): pl.pallas_call(prep_kernel, in_specs=[vmem] * 7, out_specs=[vmem] * 7, ou...  1.75 us
  transfers between devices with their start and end apart: 21, of which 7 were waited for; matrix products, arithmetic and copies ran while one was open for 3% of the time, Pallas kernels for 12%

profile of v3, /device:TPU:0, one launch (start us, length us, event | category | flops | bytes accessed | tf_op | source)
XLA Modules:
  0.0 71.0 jit_solution(13526664122194444083)
XLA Ops:
  0.6 0.0 copy-start
  0.7 1.1 %slice_select_fusion.7 = bf16[512,256]{1,0:T(8,128)(2,1)S(1)} fusion(bf16[512,1024]{1,0:T(8,128)(2,1)} %xk_ref.1, bf16[512,1024]{1,0:T(8,128)(2,1)} %gk_ref.1, pred[]{:T(512)S(6)} %eq.7), kind=kLoop, calls=%fused_computation.7 | loop fusion | flops 131072 | bytes 786433 | tf_op jit(solution)/shard_map/jit(_where)/select_n | solution.py:378
  1.8 0.0 copy-start.1
  1.8 3.1 %collective-permute-start = (bf16[512,256]{1,0:T(8,128)(2,1)S(1)}, bf16[512,256]{1,0:T(8,128)(2,1)S(1)}, u32[]{:S(2)}, u32[]{:S(2)}) collective-permute-start(bf16[512,256]{1,0:T(8,128)(2,1)S(1)} %slice_select_fusion.7), channel_id=1, source_target_pairs={{0,4},{4,0},{8,12},{12,8},{16,20},{20,16},{24,28},{28,24},{1,5},{5... | collective-permute-start | bytes 786440 | tf_op jit(solution)/shard_map/ppermute | solution.py:18
  4.9 1.1 %slice_select_fusion.6 = bf16[512,256]{1,0:T(8,128)(2,1)S(1)} fusion(bf16[512,1024]{1,0:T(8,128)(2,1)} %xk_ref.1, bf16[512,1024]{1,0:T(8,128)(2,1)} %gk_ref.1, pred[]{:T(512)S(6)} %eq.7), kind=kLoop, calls=%fused_computation.6 | loop fusion | flops 131072 | bytes 786433 | tf_op jit(solution)/shard_map/jit(_where)/select_n | solution.py:378
  6.0 0.2 collective-permute-start.1
  6.1 1.1 %broadcast_select_fusion.2 = (bf16[512,256]{1,0:T(8,128)(2,1)S(1)}, bf16[512,256]{1,0:T(8,128)(2,1)S(1)}) fusion(pred[]{:T(512)S(6)} %eq.8, bf16[512,1024]{1,0:T(8,128)(2,1)S(1)} %copy-done, pred[]{:T(512)S(6)} %eq.7, bf16[512,1024]{1,0:T(8,128)(2,1)} %gk_ref.1), kind=kLoop, calls=%fused_computation.10 | loop fusion | flops 524288 | bytes 1572866 | tf_op jit(solution)/shard_map/jit(_where)/select_n | solution.py:391
  7.2 2.1 %collective-permute-start.7 = (bf16[512,256]{1,0:T(8,128)(2,1)S(1)}, bf16[512,256]{1,0:T(8,128)(2,1)S(1)}, u32[]{:S(2)}, u32[]{:S(2)}) collective-permute-start(bf16[512,256]{1,0:T(8,128)(2,1)S(1)} %get-tuple-element.77), channel_id=1, source_target_pairs={{0,8},{4,12},{8,0},{12,4},{16,24},{20,28},{24,16},{28,20},{1,9},{5... | collective-permute-start | bytes 786440 | tf_op jit(solution)/shard_map/ppermute | solution.py:18
  9.3 0.7 collective-permute-start.8
  9.9 0.0 copy-done.1
  9.9 0.0 copy-start.12
  10.0 0.1 broadcast_select_fusion
  10.0 0.0 copy-start.11
  10.1 0.0 copy-start.2
  10.1 0.0 copy-start.3
  10.1 0.0 copy-start.4
  10.1 0.0 copy-start.8
  10.1 0.0 copy-start.9
  10.1 0.1 slice_select_fusion
  10.2 1.9 %collective-permute-done.e1_ref = bf16[512,256]{1,0:T(8,128)(2,1)S(1)} collective-permute-done((bf16[512,256]{1,0:T(8,128)(2,1)S(1)}, bf16[512,256]{1,0:T(8,128)(2,1)S(1)}, u32[]{:S(2)}, u32[]{:S(2)}) %collective-permute-start) | collective-permute-done | bytes 262176 | tf_op jit(solution)/shard_map/ppermute | solution.py:18
  12.0 2.0 %collective-permute-start.6 = (bf16[512,256]{1,0:T(8,128)(2,1)S(1)}, bf16[512,256]{1,0:T(8,128)(2,1)S(1)}, u32[]{:S(2)}, u32[]{:S(2)}) collective-permute-start(bf16[512,256]{1,0:T(8,128)(2,1)S(1)} %get-tuple-element.53), channel_id=1, source_target_pairs={{0,4},{4,0},{8,12},{12,8},{16,20},{20,16},{24,28},{28,24},{1,5},{5... | collective-permute-start | bytes 786440 | tf_op jit(solution)/shard_map/ppermute | solution.py:18
  14.1 4.0 %collective-permute-start.9 = (bf16[512,256]{1,0:T(8,128)(2,1)S(1)}, bf16[512,256]{1,0:T(8,128)(2,1)S(1)}, u32[]{:S(2)}, u32[]{:S(2)}) collective-permute-start(bf16[512,256]{1,0:T(8,128)(2,1)S(1)} %collective-permute-done.e1_ref), channel_id=1, source_target_pairs={{0,8},{8,16},{16,24},{12,4},{20,12},{28,20},{1,9},{9,17},{17,25},{... | collective-permute-start | bytes 786440 | tf_op jit(solution)/shard_map/ppermute | solution.py:406
  18.1 0.0 collective-permute-done.1.e1_ref
  18.1 1.7 %collective-permute-start.3 = (bf16[512,256]{1,0:T(8,128)(2,1)S(1)}, bf16[512,256]{1,0:T(8,128)(2,1)S(1)}, u32[]{:S(2)}, u32[]{:S(2)}) collective-permute-start(bf16[512,256]{1,0:T(8,128)(2,1)S(1)} %get-tuple-element.75), channel_id=1, source_target_pairs={{0,8},{4,12},{8,0},{12,4},{16,24},{20,28},{24,16},{28,20},{1,9},{5... | collective-permute-start | bytes 786440 | tf_op jit(solution)/shard_map/ppermute | solution.py:18
  19.8 0.6 copy-done.5
  20.4 0.0 copy-done.6
  20.4 0.0 copy-done.7
  20.4 1.7 %prep.1 = (bf16[256,1536]{1,0:T(8,128)(2,1)S(1)}, f32[64,1536]{1,0:T(8,128)S(1)}, f32[64,1536]{1,0:T(8,128)S(1)}, f32[64,1536]{1,0:T(8,128)S(1)}, f32[64,1536]{1...) custom-call(f32[17,64]{1,0:T(8,128)S(1)} %copy-done.4, f32[1,64]{1,0:T(1,128)S(1)} %bitcast.10, ...), custom_call_target="tpu_custom_call" | custom-call | tf_op jit(solution)/shard_map/prep/pallas_call | solution.py:414
  22.2 0.0 collective-permute-done.7.za_ref
  22.2 0.7 collective-permute-start.4
  22.9 0.0 collective-permute-done.8.zb_ref
  22.9 1.6 %collective-permute-start.2 = (bf16[512,256]{1,0:T(8,128)(2,1)S(1)}, bf16[512,256]{1,0:T(8,128)(2,1)S(1)}, u32[]{:S(2)}, u32[]{:S(2)}) collective-permute-start(bf16[512,256]{1,0:T(8,128)(2,1)S(1)} %get-tuple-element.50), channel_id=1, source_target_pairs={{0,4},{4,0},{8,12},{12,8},{16,20},{20,16},{24,28},{28,24},{1,5},{5... | collective-permute-start | bytes 786440 | tf_op jit(solution)/shard_map/ppermute | solution.py:18
  24.5 0.0 collective-permute-done.6.e2_ref
  24.5 6.3 %collective-permute-start.5 = (bf16[512,256]{1,0:T(8,128)(2,1)S(1)}, bf16[512,256]{1,0:T(8,128)(2,1)S(1)}, u32[]{:S(2)}, u32[]{:S(2)}) collective-permute-start(bf16[512,256]{1,0:T(8,128)(2,1)S(1)} %collective-permute-done.1.e1_ref), channel_id=1, source_target_pairs={{0,8},{8,16},{16,24},{12,4},{20,12},{28,20},{1,9},{9,17},{17,25},{... | collective-permute-start | bytes 786440 | tf_op jit(solution)/shard_map/ppermute | solution.py:406
  30.8 0.0 collective-permute-done.9.s3_ref
  30.8 7.1 %filter_grad.2 = (f32[72,256]{1,0:T(8,128)S(1)}, f32[64,1536]{1,0:T(8,128)S(1)}) custom-call(bf16[512,1024]{1,0:T(8,128)(2,1)S(1)} %copy-done, bf16[512,1024]{1,0:T(8,128)(2,1)S(1)} %copy-done.1, bf16[512,256]{1,0:T(8,128)(2,1)S(1)} %collective-permute-done.e1_ref, bf16[512,256]{1,0:T(8,128)(2,1)S(1)} %collective-permute-done.6.e2_ref, ...), custom_call_target="tpu_custom_call" | custom-call | flops 4000000000 | bytes 8388608 | tf_op jit(solution)/shard_map/filter_grad/pallas_call | solution.py:492
  38.0 0.0 collective-permute-done.3.za_ref
  38.0 0.0 collective-permute-done.4.zb_ref
  38.0 0.0 collective-permute-done.2.e2_ref
  38.0 0.0 collective-permute-done.5.s3_ref
  38.0 7.9 %filter_grad.3 = (f32[72,256]{1,0:T(8,128)S(1)}, f32[64,128]{1,0:T(8,128)S(1)}) custom-call(bf16[512,1024]{1,0:T(8,128)(2,1)S(1)} %copy-done, bf16[512,1024]{1,0:T(8,128)(2,1)S(1)} %copy-done.1, bf16[512,256]{1,0:T(8,128)(2,1)S(1)} %collective-permute-done.1.e1_ref, bf16[512,256]{1,0:T(8,128)(2,1)S(1)} %collective-permute-done.2.e2_ref, ...), custom_call_target="tpu_custom_call" | custom-call | flops 4000000000 | bytes 8388608 | tf_op jit(solution)/shard_map/filter_grad/pallas_call | solution.py:492
  45.9 0.1 collective-permute-start.18
  46.0 2.0 %collective-permute-start.15 = (f32[72,256]{1,0:T(8,128)S(1)}, f32[72,256]{1,0:T(8,128)S(1)}, u32[]{:S(2)}, u32[]{:S(2)}) collective-permute-start(f32[72,256]{1,0:T(8,128)S(1)} %get-tuple-element.62), channel_id=1, source_target_pairs={{0,8},{4,12},{8,0},{12,4},{16,24},{20,28},{24,16},{28,20},{1,9},{5... | collective-permute-start | bytes 221192 | tf_op jit(solution)/shard_map/ppermute | solution.py:18
  48.0 0.0 collective-permute-start.10
  48.0 2.3 %collective-permute-done.18 = f32[72,256]{1,0:T(8,128)S(1)} collective-permute-done((f32[72,256]{1,0:T(8,128)S(1)}, f32[72,256]{1,0:T(8,128)S(1)}, u32[]{:S(2)}, u32[]{:S(2)}) %collective-permute-start.18) | collective-permute-done | bytes 73760 | tf_op jit(solution)/shard_map/ppermute | solution.py:18
  50.4 0.5 collective-permute-start.19
  50.9 0.3 collective-permute-done.15
  51.2 2.3 %collective-permute-start.16 = (f32[72,256]{1,0:T(8,128)S(1)}, f32[72,256]{1,0:T(8,128)S(1)}, u32[]{:S(2)}, u32[]{:S(2)}) collective-permute-start(f32[72,256]{1,0:T(8,128)S(1)} %add.38), channel_id=1, source_target_pairs={{0,16},{4,20},{8,24},{12,28},{16,0},{20,4},{24,8},{28,12},{1,17},{... | collective-permute-start | bytes 221192 | tf_op jit(solution)/shard_map/ppermute | solution.py:18
  53.4 0.0 collective-permute-done.10
  53.4 1.6 %collective-permute-start.11 = (f32[64,128]{1,0:T(8,128)S(1)}, f32[64,128]{1,0:T(8,128)S(1)}, u32[]{:S(2)}, u32[]{:S(2)}) collective-permute-start(f32[64,128]{1,0:T(8,128)S(1)} %add.34), channel_id=1, source_target_pairs={{0,2},{1,3},{2,0},{3,1},{4,6},{5,7},{6,4},{7,5},{8,10},{9,11},{10,... | collective-permute-start | bytes 98312 | tf_op jit(solution)/shard_map/ppermute | solution.py:18
  55.0 2.4 %collective-permute-done.11 = f32[64,128]{1,0:T(8,128)S(1)} collective-permute-done((f32[64,128]{1,0:T(8,128)S(1)}, f32[64,128]{1,0:T(8,128)S(1)}, u32[]{:S(2)}, u32[]{:S(2)}) %collective-permute-start.11) | collective-permute-done | bytes 32800 | tf_op jit(solution)/shard_map/ppermute | solution.py:18
  57.4 0.0 collective-permute-start.12
  57.4 0.0 collective-permute-done.19
  57.5 2.1 %collective-permute-start.20 = (f32[72,256]{1,0:T(8,128)S(1)}, f32[72,256]{1,0:T(8,128)S(1)}, u32[]{:S(2)}, u32[]{:S(2)}) collective-permute-start(f32[72,256]{1,0:T(8,128)S(1)} %add.41.rest_2_), channel_id=1, source_target_pairs={{0,4},{4,0},{8,12},{12,8},{16,20},{20,16},{24,28},{28,24},{1,5},{5... | collective-permute-start | bytes 221192 | tf_op jit(solution)/shard_map/ppermute | solution.py:18
  59.5 0.0 collective-permute-done.16
  59.6 0.1 collective-permute-start.17
  59.7 1.7 %collective-permute-done.12 = f32[64,128]{1,0:T(8,128)S(1)} collective-permute-done((f32[64,128]{1,0:T(8,128)S(1)}, f32[64,128]{1,0:T(8,128)S(1)}, u32[]{:S(2)}, u32[]{:S(2)}) %collective-permute-start.12) | collective-permute-done | bytes 32800 | tf_op jit(solution)/shard_map/ppermute | solution.py:18
  61.4 0.3 collective-permute-start.13
  61.6 3.6 %collective-permute-done.13 = f32[64,128]{1,0:T(8,128)S(1)} collective-permute-done((f32[64,128]{1,0:T(8,128)S(1)}, f32[64,128]{1,0:T(8,128)S(1)}, u32[]{:S(2)}, u32[]{:S(2)}) %collective-permute-start.13) | collective-permute-done | bytes 32800 | tf_op jit(solution)/shard_map/ppermute | solution.py:18
  65.3 0.7 collective-permute-start.14
  66.0 4.2 %collective-permute-done.14.far_ref = f32[64,128]{1,0:T(8,128)S(1)} collective-permute-done((f32[64,128]{1,0:T(8,128)S(1)}, f32[64,128]{1,0:T(8,128)S(1)}, u32[]{:S(2)}, u32[]{:S(2)}) %collective-permute-start.14) | collective-permute-done | bytes 32800 | tf_op jit(solution)/shard_map/ppermute | solution.py:18
  70.1 0.0 collective-permute-done.20.rest_3_
  70.1 0.0 collective-permute-done.17.rest_1_
  70.1 0.8 %finish.1 = (f32[17,64]{1,0:T(8,128)}, f32[1,64]{1,0:T(1,128)}, f32[1,64]{1,0:T(1,128)}, f32[64,64]{1,0:T(8,128)}, f32[1,64]{1,0:T(1,128)}, /*index=5*/f32[1,64]...) custom-call(f32[64,128]{1,0:T(8,128)S(1)} %add.37.net_ref, f32[64,128]{1,0:T(8,128)S(1)} %collective-permute-done.14.far_ref, ...), custom_call_target="tpu_custom_call" | custom-call | tf_op jit(solution)/shard_map/finish/pallas_call | solution.py:523
  (21 shorter events, 0.1 us)
Async XLA Ops:
  0.6 5.5 %copy-start = (bf16[512,1024]{1,0:T(8,128)(2,1)S(1)}, bf16[512,1024]{1,0:T(8,128)(2,1)}, u32[]{:S(2)}) copy-start(bf16[512,1024]{1,0:T(8,128)(2,1)} %xk_ref.1) | copy-start | bytes 3145732
  1.8 8.1 %copy-start.1 = (bf16[512,1024]{1,0:T(8,128)(2,1)S(1)}, bf16[512,1024]{1,0:T(8,128)(2,1)}, u32[]{:S(2)}) copy-start(bf16[512,1024]{1,0:T(8,128)(2,1)} %gk_ref.1) | copy-start | bytes 3145732
  1.8 10.2 %collective-permute-start = (bf16[512,256]{1,0:T(8,128)(2,1)S(1)}, bf16[512,256]{1,0:T(8,128)(2,1)S(1)}, u32[]{:S(2)}, u32[]{:S(2)}) collective-permute-start(bf16[512,256]{1,0:T(8,128)(2,1)S(1)} %slice_select_fusion.7), channel_id=1, source_target_pairs={{0,4},{4,0},{8,12},{12,8},{16,20},{20,16},{24,28},{28,24},{1,5},{5... | collective-permute-start | bytes 786440 | tf_op jit(solution)/shard_map/ppermute | solution.py:18
  6.0 12.1 %collective-permute-start.1 = (bf16[512,256]{1,0:T(8,128)(2,1)S(1)}, bf16[512,256]{1,0:T(8,128)(2,1)S(1)}, u32[]{:S(2)}, u32[]{:S(2)}) collective-permute-start(bf16[512,256]{1,0:T(8,128)(2,1)S(1)} %slice_select_fusion.6), channel_id=1, source_target_pairs={{0,4},{4,0},{8,12},{12,8},{16,20},{20,16},{24,28},{28,24},{1,5},{5... | collective-permute-start | bytes 786440 | tf_op jit(solution)/shard_map/ppermute | solution.py:18
  7.2 15.0 %collective-permute-start.7 = (bf16[512,256]{1,0:T(8,128)(2,1)S(1)}, bf16[512,256]{1,0:T(8,128)(2,1)S(1)}, u32[]{:S(2)}, u32[]{:S(2)}) collective-permute-start(bf16[512,256]{1,0:T(8,128)(2,1)S(1)} %get-tuple-element.77), channel_id=1, source_target_pairs={{0,8},{4,12},{8,0},{12,4},{16,24},{20,28},{24,16},{28,20},{1,9},{5... | collective-permute-start | bytes 786440 | tf_op jit(solution)/shard_map/ppermute | solution.py:18
  9.3 13.6 %collective-permute-start.8 = (bf16[512,256]{1,0:T(8,128)(2,1)S(1)}, bf16[512,256]{1,0:T(8,128)(2,1)S(1)}, u32[]{:S(2)}, u32[]{:S(2)}) collective-permute-start(bf16[512,256]{1,0:T(8,128)(2,1)S(1)} %get-tuple-element.76), channel_id=1, source_target_pairs={{8,16},{12,20},{16,8},{20,12},{9,17},{13,21},{17,9},{21,13},{10,18... | collective-permute-start | bytes 786440 | tf_op jit(solution)/shard_map/ppermute | solution.py:402
  9.9 20.8 %copy-start.12 = (bf16[2,256,256]{2,1,0:T(8,128)(2,1)S(1)}, bf16[2,256,256]{2,1,0:T(8,128)(2,1)}, u32[]{:S(2)}) copy-start(bf16[2,256,256]{2,1,0:T(8,128)(2,1)} %constant.43.clone.inv_ref) | copy-start | bytes 786436
  10.0 20.8 %copy-start.11 = (bf16[2,1024,256]{2,1,0:T(8,128)(2,1)S(1)}, bf16[2,1024,256]{2,1,0:T(8,128)(2,1)}, u32[]{:S(2)}) copy-start(bf16[2,1024,256]{2,1,0:T(8,128)(2,1)} %constant.42.clone.fwd_ref) | copy-start | bytes 3145732
  10.1 9.7 %copy-start.2 = (f32[17,1536]{1,0:T(8,128)S(1)}, f32[17,1536]{1,0:T(8,128)}, u32[]{:S(2)}) copy-start(f32[17,1536]{1,0:T(8,128)} %constant.41.clone.feats_ref.rest_3_) | copy-start | bytes 313348
  10.1 9.7 %copy-start.3 = (f32[64,64]{1,0:T(8,128)S(1)}, f32[64,64]{1,0:T(8,128)}, u32[]{:S(2)}) copy-start(f32[64,64]{1,0:T(8,128)} %rest_1_.1) | copy-start | bytes 49156
  10.1 9.7 %copy-start.4 = (f32[17,64]{1,0:T(8,128)S(1)}, f32[17,64]{1,0:T(8,128)}, u32[]{:S(2)}) copy-start(f32[17,64]{1,0:T(8,128)} %ew_ref) | copy-start | bytes 13060
  10.1 9.7 %copy-start.8 = (f32[64]{0:T(128)S(1)}, f32[64]{0:T(128)}, u32[]{:S(2)}) copy-start(f32[64]{0:T(128)} %param.20) | copy-start | bytes 772
  10.1 20.7 %copy-start.9 = (f32[64,1024]{1,0:T(8,128)S(1)}, f32[64,1024]{1,0:T(8,128)}, u32[]{:S(2)}) copy-start(f32[64,1024]{1,0:T(8,128)} %head_ref.3) | copy-start | bytes 786436
  12.0 12.4 %collective-permute-start.6 = (bf16[512,256]{1,0:T(8,128)(2,1)S(1)}, bf16[512,256]{1,0:T(8,128)(2,1)S(1)}, u32[]{:S(2)}, u32[]{:S(2)}) collective-permute-start(bf16[512,256]{1,0:T(8,128)(2,1)S(1)} %get-tuple-element.53), channel_id=1, source_target_pairs={{0,4},{4,0},{8,12},{12,8},{16,20},{20,16},{24,28},{28,24},{1,5},{5... | collective-permute-start | bytes 786440 | tf_op jit(solution)/shard_map/ppermute | solution.py:18
  14.1 16.7 %collective-permute-start.9 = (bf16[512,256]{1,0:T(8,128)(2,1)S(1)}, bf16[512,256]{1,0:T(8,128)(2,1)S(1)}, u32[]{:S(2)}, u32[]{:S(2)}) collective-permute-start(bf16[512,256]{1,0:T(8,128)(2,1)S(1)} %collective-permute-done.e1_ref), channel_id=1, source_target_pairs={{0,8},{8,16},{16,24},{12,4},{20,12},{28,20},{1,9},{9,17},{17,25},{... | collective-permute-start | bytes 786440 | tf_op jit(solution)/shard_map/ppermute | solution.py:406
  18.1 19.9 %collective-permute-start.3 = (bf16[512,256]{1,0:T(8,128)(2,1)S(1)}, bf16[512,256]{1,0:T(8,128)(2,1)S(1)}, u32[]{:S(2)}, u32[]{:S(2)}) collective-permute-start(bf16[512,256]{1,0:T(8,128)(2,1)S(1)} %get-tuple-element.75), channel_id=1, source_target_pairs={{0,8},{4,12},{8,0},{12,4},{16,24},{20,28},{24,16},{28,20},{1,9},{5... | collective-permute-start | bytes 786440 | tf_op jit(solution)/shard_map/ppermute | solution.py:18
  19.7 0.7 copy-start.5
  19.7 0.7 copy-start.6
  19.7 0.7 copy-start.7
  20.4 10.4 %copy-start.10 = (f32[1024]{0:T(1024)S(1)}, f32[1024]{0:T(1024)}, u32[]{:S(2)}) copy-start(f32[1024]{0:T(1024)} %param.22) | copy-start | bytes 12292
  22.2 15.8 %collective-permute-start.4 = (bf16[512,256]{1,0:T(8,128)(2,1)S(1)}, bf16[512,256]{1,0:T(8,128)(2,1)S(1)}, u32[]{:S(2)}, u32[]{:S(2)}) collective-permute-start(bf16[512,256]{1,0:T(8,128)(2,1)S(1)} %get-tuple-element.74), channel_id=1, source_target_pairs={{8,16},{12,20},{16,8},{20,12},{9,17},{13,21},{17,9},{21,13},{10,18... | collective-permute-start | bytes 786440 | tf_op jit(solution)/shard_map/ppermute | solution.py:402
  22.9 15.1 %collective-permute-start.2 = (bf16[512,256]{1,0:T(8,128)(2,1)S(1)}, bf16[512,256]{1,0:T(8,128)(2,1)S(1)}, u32[]{:S(2)}, u32[]{:S(2)}) collective-permute-start(bf16[512,256]{1,0:T(8,128)(2,1)S(1)} %get-tuple-element.50), channel_id=1, source_target_pairs={{0,4},{4,0},{8,12},{12,8},{16,20},{20,16},{24,28},{28,24},{1,5},{5... | collective-permute-start | bytes 786440 | tf_op jit(solution)/shard_map/ppermute | solution.py:18
  24.5 13.5 %collective-permute-start.5 = (bf16[512,256]{1,0:T(8,128)(2,1)S(1)}, bf16[512,256]{1,0:T(8,128)(2,1)S(1)}, u32[]{:S(2)}, u32[]{:S(2)}) collective-permute-start(bf16[512,256]{1,0:T(8,128)(2,1)S(1)} %collective-permute-done.1.e1_ref), channel_id=1, source_target_pairs={{0,8},{8,16},{16,24},{12,4},{20,12},{28,20},{1,9},{9,17},{17,25},{... | collective-permute-start | bytes 786440 | tf_op jit(solution)/shard_map/ppermute | solution.py:406
  45.9 4.4 %collective-permute-start.18 = (f32[72,256]{1,0:T(8,128)S(1)}, f32[72,256]{1,0:T(8,128)S(1)}, u32[]{:S(2)}, u32[]{:S(2)}) collective-permute-start(f32[72,256]{1,0:T(8,128)S(1)} %get-tuple-element.63), channel_id=1, source_target_pairs={{0,8},{4,12},{8,0},{12,4},{16,24},{20,28},{24,16},{28,20},{1,9},{5... | collective-permute-start | bytes 221192 | tf_op jit(solution)/shard_map/ppermute | solution.py:18
  46.0 5.1 %collective-permute-start.15 = (f32[72,256]{1,0:T(8,128)S(1)}, f32[72,256]{1,0:T(8,128)S(1)}, u32[]{:S(2)}, u32[]{:S(2)}) collective-permute-start(f32[72,256]{1,0:T(8,128)S(1)} %get-tuple-element.62), channel_id=1, source_target_pairs={{0,8},{4,12},{8,0},{12,4},{16,24},{20,28},{24,16},{28,20},{1,9},{5... | collective-permute-start | bytes 221192 | tf_op jit(solution)/shard_map/ppermute | solution.py:18
  48.0 5.4 %collective-permute-start.10 = (f32[64,128]{1,0:T(8,128)S(1)}, f32[64,128]{1,0:T(8,128)S(1)}, u32[]{:S(2)}, u32[]{:S(2)}) collective-permute-start(f32[64,128]{1,0:T(8,128)S(1)} %get-tuple-element.61), channel_id=1, source_target_pairs={{0,1},{1,0},{2,3},{3,2},{4,5},{5,4},{6,7},{7,6},{8,9},{9,8},{10,11... | collective-permute-start | bytes 98312 | tf_op jit(solution)/shard_map/ppermute | solution.py:18
  50.4 7.1 %collective-permute-start.19 = (f32[72,256]{1,0:T(8,128)S(1)}, f32[72,256]{1,0:T(8,128)S(1)}, u32[]{:S(2)}, u32[]{:S(2)}) collective-permute-start(f32[72,256]{1,0:T(8,128)S(1)} %add.40), channel_id=1, source_target_pairs={{0,16},{4,20},{8,24},{12,28},{16,0},{20,4},{24,8},{28,12},{1,17},{... | collective-permute-start | bytes 221192 | tf_op jit(solution)/shard_map/ppermute | solution.py:18
  51.2 8.4 %collective-permute-start.16 = (f32[72,256]{1,0:T(8,128)S(1)}, f32[72,256]{1,0:T(8,128)S(1)}, u32[]{:S(2)}, u32[]{:S(2)}) collective-permute-start(f32[72,256]{1,0:T(8,128)S(1)} %add.38), channel_id=1, source_target_pairs={{0,16},{4,20},{8,24},{12,28},{16,0},{20,4},{24,8},{28,12},{1,17},{... | collective-permute-start | bytes 221192 | tf_op jit(solution)/shard_map/ppermute | solution.py:18
  53.4 4.0 %collective-permute-start.11 = (f32[64,128]{1,0:T(8,128)S(1)}, f32[64,128]{1,0:T(8,128)S(1)}, u32[]{:S(2)}, u32[]{:S(2)}) collective-permute-start(f32[64,128]{1,0:T(8,128)S(1)} %add.34), channel_id=1, source_target_pairs={{0,2},{1,3},{2,0},{3,1},{4,6},{5,7},{6,4},{7,5},{8,10},{9,11},{10,... | collective-permute-start | bytes 98312 | tf_op jit(solution)/shard_map/ppermute | solution.py:18
  57.4 3.9 %collective-permute-start.12 = (f32[64,128]{1,0:T(8,128)S(1)}, f32[64,128]{1,0:T(8,128)S(1)}, u32[]{:S(2)}, u32[]{:S(2)}) collective-permute-start(f32[64,128]{1,0:T(8,128)S(1)} %add.35), channel_id=1, source_target_pairs={{0,4},{4,0},{8,12},{12,8},{16,20},{20,16},{24,28},{28,24},{1,5},{5... | collective-permute-start | bytes 98312 | tf_op jit(solution)/shard_map/ppermute | solution.py:18
  57.5 12.7 %collective-permute-start.20 = (f32[72,256]{1,0:T(8,128)S(1)}, f32[72,256]{1,0:T(8,128)S(1)}, u32[]{:S(2)}, u32[]{:S(2)}) collective-permute-start(f32[72,256]{1,0:T(8,128)S(1)} %add.41.rest_2_), channel_id=1, source_target_pairs={{0,4},{4,0},{8,12},{12,8},{16,20},{20,16},{24,28},{28,24},{1,5},{5... | collective-permute-start | bytes 221192 | tf_op jit(solution)/shard_map/ppermute | solution.py:18
  59.6 10.6 %collective-permute-start.17 = (f32[72,256]{1,0:T(8,128)S(1)}, f32[72,256]{1,0:T(8,128)S(1)}, u32[]{:S(2)}, u32[]{:S(2)}) collective-permute-start(f32[72,256]{1,0:T(8,128)S(1)} %add.39.rest_0_), channel_id=1, source_target_pairs={{0,4},{4,0},{8,12},{12,8},{16,20},{20,16},{24,28},{28,24},{1,5},{5... | collective-permute-start | bytes 221192 | tf_op jit(solution)/shard_map/ppermute | solution.py:18
  61.4 3.9 %collective-permute-start.13 = (f32[64,128]{1,0:T(8,128)S(1)}, f32[64,128]{1,0:T(8,128)S(1)}, u32[]{:S(2)}, u32[]{:S(2)}) collective-permute-start(f32[64,128]{1,0:T(8,128)S(1)} %add.36), channel_id=1, source_target_pairs={{0,8},{4,12},{8,0},{12,4},{16,24},{20,28},{24,16},{28,20},{1,9},{5... | collective-permute-start | bytes 98312 | tf_op jit(solution)/shard_map/ppermute | solution.py:18
  65.3 4.9 %collective-permute-start.14 = (f32[64,128]{1,0:T(8,128)S(1)}, f32[64,128]{1,0:T(8,128)S(1)}, u32[]{:S(2)}, u32[]{:S(2)}) collective-permute-start(f32[64,128]{1,0:T(8,128)S(1)} %add.37.net_ref), channel_id=1, source_target_pairs={{0,16},{4,20},{8,24},{12,28},{16,0},{20,4},{24,8},{28,12},{1,17},{... | collective-permute-start | bytes 98312 | tf_op jit(solution)/shard_map/ppermute | solution.py:18
